TPU v7x, 256 devices: a whole 4x4x8 slice. The times are simulated.
256 devices in a mesh: row: 8 (over y, core), col: 4 (over x), layer: 8 (over z).
Axes of the slice: x: 4, y: 4, z: 8, core: 2. Of those that a mesh axis runs over, the one named last changes fastest.
Arguments:
- a_vals: bfloat16 [192, 8, 8, 64, 128], P('row', 'layer', 'col'), may hold values from -0.375 to 0.375
- a_cols: int32 [192, 8, 8, 2], P('row', 'layer', 'col'), may hold values from 0 to 7, as said below
- a_count: int32 [192, 8, 8], P('row', 'layer', 'col'), may hold values from 0 to 2, as said below
- panel_map: int32 [8, 8], replicated, may hold values from 0 to 7, each once within a row
- p_vals: bfloat16 [8, 8, 8, 4, 64, 256], P('layer', 'row', None, 'col'), may hold values from -6 to 6
- p_cols: int32 [8, 8, 8, 4, 4], P('layer', 'row', None, 'col'), may hold values from 0 to 7, as said below
- p_count: int32 [8, 8, 8, 4], P('layer', 'row', None, 'col'), may hold values from 0 to 4, as said below
Outputs:
- product: bfloat16 [12288, 2048], P(('row', 'col', 'layer'))
Inputs may be any that keep to these rules, and one draw needn't show every extreme that they name: `a_count`: each block row has at most 27 valid operator blocks in all, some block row exactly 27, and some entry reaches 2. `a_cols`: the slots of one block row and section name distinct block columns. `p_cols`: the slots of one block row and group name distinct coarse columns. `p_count`: reaches 4 somewhere in every draw.
All inputs are finite; a program needn't handle non-finite values.
Results may differ from a plain program's by a relative error of at most 0.001.
Values may be sent and summed in bfloat16 or wider, within the bound.
No kernel may reach another device: no remote copies, remote signals or barrier semaphores. Data moves between devices by JAX's collectives and lax.ppermute only.
A program may use at most 128 MiB of HBM per device.

v0:
```python
import jax
import jax.numpy as jnp
from jax import lax
from jax.sharding import PartitionSpec as P

CB = 8


def expand(blocks, cols, count):
    panel_rows, groups, block_side, wide = blocks.shape
    slot_count = cols.shape[2]
    pieces_view = blocks.reshape(panel_rows, groups, block_side, slot_count, block_side)
    valid_mask = jnp.arange(slot_count)[None, None, :] < count[:, :, None]
    onehot = (
        (cols[:, :, :, None] == jnp.arange(CB)[None, None, None, :]) & valid_mask[:, :, :, None]
    ).astype(jnp.bfloat16)
    dense_rows = jnp.einsum(
        "kgytz,kgtc->kygcz", pieces_view, onehot, preferred_element_type=jnp.float32
    )
    return dense_rows.astype(jnp.bfloat16).reshape(panel_rows, block_side, groups * CB * block_side)


def accumulate(running, a_panel, a_cols_panel, a_count_panel, dense_rows):
    rows_blk, block_side, wide = a_panel.shape
    slot_count = a_cols_panel.shape[1]
    valid_mask = (jnp.arange(slot_count)[None, :] < a_count_panel[:, None]).astype(jnp.bfloat16)
    masked = (
        a_panel.reshape(rows_blk, block_side, slot_count, block_side) * valid_mask[:, None, :, None]
    ).reshape(rows_blk, block_side, wide)
    picked = jnp.take(dense_rows, a_cols_panel, axis=0).reshape(
        rows_blk, slot_count * block_side, dense_rows.shape[2]
    )
    return running + jnp.einsum("ixk,ikn->ixn", masked, picked, preferred_element_type=jnp.float32)


def pick_panel(array, panel_idx):
    return lax.dynamic_index_in_dim(array, panel_idx, 0, keepdims=False)


def body(a_vals, a_cols, a_count, panel_map, p_vals, p_cols, p_count):
    rows_blk = a_vals.shape[0]
    block_side = a_vals.shape[3]
    held_sections = a_vals.shape[2]
    layer_map = lax.dynamic_index_in_dim(panel_map, lax.axis_index("layer"), 0, keepdims=False)
    section_vals, section_cols, section_count = (
        lax.all_gather(p_vals, "row", axis=1, tiled=True),
        lax.all_gather(p_cols, "row", axis=1, tiled=True),
        lax.all_gather(p_count, "row", axis=1, tiled=True),
    )
    full_vals, full_cols, full_count = (
        lax.all_gather(section_vals, "col", axis=3, tiled=True),
        lax.all_gather(section_cols, "col", axis=3, tiled=True),
        lax.all_gather(section_count, "col", axis=3, tiled=True),
    )
    width_all = full_vals.shape[3] * CB * block_side
    running = jnp.zeros((rows_blk, block_side, width_all), jnp.float32)
    first_section = lax.axis_index("col") * held_sections
    for section_slot in range(held_sections):
        panel_idx = pick_panel(layer_map, first_section + section_slot)
        dense_rows = expand(
            pick_panel(full_vals[0], panel_idx),
            pick_panel(full_cols[0], panel_idx),
            pick_panel(full_count[0], panel_idx),
        )
        running = accumulate(
            running,
            a_vals[:, 0, section_slot],
            a_cols[:, 0, section_slot],
            a_count[:, 0, section_slot],
            dense_rows,
        )
    partial_terms = running.reshape(rows_blk * block_side, width_all)
    return lax.psum_scatter(
        partial_terms, ("col", "layer"), scatter_dimension=0, tiled=True
    ).astype(jnp.bfloat16)


def solution(mesh):
    placed = (
        P("row", "layer", "col", None, None),
        P("row", "layer", "col", None),
        P("row", "layer", "col"),
        P(),
        P("layer", "row", None, "col", None, None),
        P("layer", "row", None, "col", None),
        P("layer", "row", None, "col"),
    )
    return jax.shard_map(
        body,
        mesh=mesh,
        in_specs=placed,
        out_specs=P(("row", "col", "layer"), None),
        check_vma=False,
    )
```

profile of v0, /device:TPU:8, one launch (start us, length us, event | category | flops | bytes accessed | tf_op | source)
XLA Modules:
  0.0 456.4 jit_solution(16191405990776112186)
XLA Ops:
  7.3 31.6 %all-gather.3.cloned.1.call-done = bf16[1,8,8,1,64,256]{5,4,3,2,0,1:T(8,128)(2,1)} async-done(((bf16[1,1,8,1,64,256]{5,4,3,2,0,1:T(8,128)(2,1)}), bf16[1,8,8,1,64,256]{5,4,3,2,0,1:T(8,128)(2,1)}) %all-gather.3.cloned.1.call-update) | async-done | bytes 2097168 | tf_op jit(solution)/shard_map/all_gather | solution.py:46
  39.0 1.4 fusion.17
  47.4 9.4 %all_gather.20 = s32[1,8,8,1]{2,3,0,1:T(1,128)S(1)} all-gather(s32[1,1,8,1]{2,3,0,1:T(1,128)} %bitcast.75), channel_id=1, replica_groups=mesh['row'=8,'col'=4,'layer'=8] {'row'}, dimensions={1}, use_global_device_ids=true | all-gather | bytes 288 | tf_op jit(solution)/shard_map/all_gather | solution.py:48
  56.8 12.2 %all_gather.21 = s32[1,8,8,4]{2,1,0,3:T(8,128)S(1)} all-gather(s32[1,8,8,1]{2,1,0,3:T(8,128)S(1)} %bitcast.71), channel_id=1, replica_groups=mesh['row'=8,'col'=4,'layer'=8] {'col'}, dimensions={3}, use_global_device_ids=true | all-gather | bytes 1280 | tf_op jit(solution)/shard_map/all_gather | solution.py:53
  69.4 11.1 %all_gather.18 = s32[1,8,8,1,4]{2,4,3,0,1:T(4,128)S(1)} all-gather(s32[1,1,8,1,4]{2,4,3,0,1:T(4,128)} %bitcast.74), channel_id=1, replica_groups=mesh['row'=8,'col'=4,'layer'=8] {'row'}, dimensions={1}, use_global_device_ids=true | all-gather | bytes 1152 | tf_op jit(solution)/shard_map/all_gather | solution.py:47
  80.5 10.8 %all_gather.19 = s32[1,8,8,4,4]{2,4,3,0,1:T(4,128)S(1)} all-gather(s32[1,8,8,1,4]{2,4,3,0,1:T(4,128)S(1)} %all_gather.18), channel_id=1, replica_groups=mesh['row'=8,'col'=4,'layer'=8] {'col'}, dimensions={3}, use_global_device_ids=true | all-gather | bytes 5120 | tf_op jit(solution)/shard_map/all_gather | solution.py:52
  91.7 37.1 %all-gather.5.cloned.1.call-done = bf16[1,8,8,4,64,256]{5,4,3,2,0,1:T(8,128)(2,1)} async-done(((bf16[1,8,8,1,64,256]{5,4,3,2,0,1:T(8,128)(2,1)}), bf16[1,8,8,4,64,256]{5,4,3,2,0,1:T(8,128)(2,1)}) %all-gather.5.cloned.1.call-update) | async-done | bytes 8388624 | tf_op jit(solution)/shard_map/all_gather | solution.py:51
  128.8 2.8 constant_dynamic-slice_fusion
  131.6 3.3 reshape.115
  134.9 1.9 convert_bitcast_fusion
  136.9 2.7 copy.38
  139.6 5.8 %reshape.116 = bf16[8,64,2048]{2,1,0:T(8,128)(2,1)S(1)} reshape(bf16[8,64,4,8,64]{4,3,2,1,0:T(8,128)(2,1)} %copy.38) | data formatting | bytes 4194304 | tf_op jit(solution)/shard_map/reshape | solution.py:20
  145.4 1.8 reshape.112
  147.2 3.1 convert_bitcast_fusion.1
  150.3 2.7 copy.33
  153.1 6.8 %reshape.113 = bf16[8,64,2048]{2,1,0:T(8,128)(2,1)} reshape(bf16[8,64,4,8,64]{4,3,2,1,0:T(8,128)(2,1)} %copy.33) | data formatting | bytes 4194304 | tf_op jit(solution)/shard_map/reshape | solution.py:20
  159.8 7.9 %gather_fusion = bf16[48,64,2048]{2,1,0:T(8,128)(2,1)} fusion(bf16[8,64,2048]{2,1,0:T(8,128)(2,1)} %reshape.113, s32[1024]{0:T(1024)S(1)} %pad_clamp_fusion.1), kind=kCustom, calls=%fused_computation.clone | custom fusion | bytes 25166016 | tf_op jit(solution)/shard_map/jit(_take)/gather | solution.py:30
  167.7 10.7 %broadcast_select_fusion.1 = bf16[24,2,64,2048]{3,2,1,0:T(8,128)(2,1)} fusion(bf16[24,2,64,2048]{3,2,1,0:T(8,128)(2,1)} %bitcast.68, pred[24,2]{1,0:T(8,128)(4,1)S(1)} %copy.26), kind=kLoop, calls=%fused_computation.3 | loop fusion | flops 6291456 | bytes 25165872 | tf_op jit(solution)/shard_map/jit(_take)/select_n | solution.py:30
  178.4 6.4 %gather_fusion.1 = bf16[48,64,2048]{2,1,0:T(8,128)(2,1)} fusion(bf16[8,64,2048]{2,1,0:T(8,128)(2,1)S(1)} %reshape.116, s32[1024]{0:T(1024)S(1)} %pad_clamp_fusion), kind=kCustom, calls=%fused_computation.1.clone | custom fusion | bytes 25166016 | tf_op jit(solution)/shard_map/jit(_take)/gather | solution.py:30
  184.8 12.5 %broadcast_select_fusion = bf16[24,2,64,2048]{3,2,1,0:T(8,128)(2,1)} fusion(bf16[24,2,64,2048]{3,2,1,0:T(8,128)(2,1)} %bitcast.69, pred[24,2]{1,0:T(8,128)(4,1)S(1)} %copy.35), kind=kLoop, calls=%fused_computation.2 | loop fusion | flops 6291456 | bytes 25165872 | tf_op jit(solution)/shard_map/jit(_take)/select_n | solution.py:30
  197.3 1.8 fusion
  199.1 11.0 %convolution_add_fusion = f32[24,64,2048]{2,1,0:T(8,128)} fusion(f32[24,64,2048]{2,1,0:T(8,128)S(1)} %fusion, bf16[24,128,2048]{2,1,0:T(8,128)(2,1)} %bitcast.66, bf16[24,1,2,64,128]{4,3,2,1,0:T(8,128)(2,1)S(1)} %copy-done.1, bf16[24,128]{1,0:T(8,128)(2,1)S(1)} %mul.35), kind=kOutput, calls=%fused_computation.4 | convolution fusion | flops 808648704 | bytes 38148096 | tf_op jit(solution)/shard_map/ixk,ikn->ixn/dot_general | solution.py:33
  210.2 238.0 %reduce-scatter.2.cloned.1.call-done = f32[48,2048]{1,0:T(8,128)} async-done(((f32[1536,2048]{1,0:T(8,128)}), f32[48,2048]{1,0:T(8,128)}) %reduce-scatter.2.cloned.1.call-update) | async-done | bytes 393232 | tf_op jit(solution)/shard_map/reduce_scatter | solution.py:73
  448.2 1.7 convert_element_type.37
  (34 shorter events, 4.5 us)
Async XLA Ops:
  6.5 32.4 %all-gather.3.cloned.1.call-start = ((), (), s32[]{:S(2)}) async-start(), calls=%async_computation.1 | async-start | bytes 2359296 | tf_op jit(solution)/shard_map/all_gather | solution.py:46
  7.3 121.6 %all-gather.5.cloned.1.call-start = ((), (), s32[]{:S(2)}) async-start(), calls=%async_computation.2 | async-start | bytes 10485760 | tf_op jit(solution)/shard_map/all_gather | solution.py:51
  39.0 409.2 %reduce-scatter.2.cloned.1.call-start = ((), (), s32[]{:S(2)}) async-start(), calls=%async_computation.3 | async-start | bytes 12976128 | tf_op jit(solution)/shard_map/reduce_scatter | solution.py:73
  184.8 12.5 %copy-start = (bf16[24,2,64,2048]{3,2,1,0:T(8,128)(2,1)S(1)}, bf16[24,2,64,2048]{3,2,1,0:T(8,128)(2,1)}, u32[]{:S(2)}) copy-start(bf16[24,2,64,2048]{3,2,1,0:T(8,128)(2,1)} %broadcast_select_fusion.1) | copy-start | bytes 37748740
  184.8 12.5 %copy-start.1 = (bf16[24,1,2,64,128]{4,3,2,1,0:T(8,128)(2,1)S(1)}, bf16[24,1,2,64,128]{4,3,2,1,0:T(8,128)(2,1)}, u32[]{:S(2)}) copy-start(bf16[24,1,2,64,128]{4,3,2,1,0:T(8,128)(2,1)} %param.9) | copy-start | bytes 2359300
Sparse Core Ops, SparseCore 0:
  9.2 29.6 all-gather.2
  40.7 88.0 all-gather.4
  210.3 237.8 reduce-scatter.1
where the time goes:
time: 457 us; the launch traced here: 456 us
  waiting for transfers between devices  307 us (67%)
  local copies, waits for them, and re-layouts  43.6 us (10%)
  blocking collectives  43.5 us (10%)
  other arithmetic  26.6 us (6%)
  matrix products  17.9 us (4%)
  between operations  17.2 us (4%)
    reduce_scatter x1, waiting for transfers between devices, body(): lax.psum_scatter(partial_terms, ('col', 'layer'), scatter_dimension=0, ti...  238 us
    all_gather x1, waiting for transfers between devices, body(): lax.all_gather(section_vals, 'col', axis=3, tiled=True)  37.1 us
    all_gather x1, waiting for transfers between devices, body(): lax.all_gather(p_vals, 'row', axis=1, tiled=True)  31.6 us
    select_n x3, other arithmetic, accumulate(): jnp.take(dense_rows, a_cols_panel, axis=0)  24 us
    gather x2, local copies, waits for them, and re-layouts, accumulate(): jnp.take(dense_rows, a_cols_panel, axis=0)  14.2 us
    dot_general x2, matrix products, accumulate(): jnp.einsum('ixk,ikn->ixn', masked, picked, preferred_element_type=jnp.flo...  12.8 us
    reshape x2, local copies, waits for them, and re-layouts, expand(): dense_rows.astype(jnp.bfloat16)  12.5 us
    all_gather x1, blocking collectives, body(): lax.all_gather(section_count, 'col', axis=3, tiled=True)  12.2 us
  transfers between devices with their start and end apart: 3, of which 3 were waited for; matrix products, arithmetic and copies ran while one was open for 1% of the time, Pallas kernels for 0%

commit v1 on v0

v1 whole, which is shorter than its diff:
```python
import functools

import jax
import jax.numpy as jnp
from jax import lax
from jax.experimental import pallas as pl
from jax.experimental.pallas import tpu as pltpu
from jax.sharding import PartitionSpec as P

CB = 8
BF = jnp.bfloat16
F32 = jnp.float32


def expand_kernel(col_ref, p_ref, out_ref):
    lane = lax.broadcasted_iota(jnp.int32, (16, 128), 1)
    low = lane < 64
    panel_rows = p_ref.shape[1] // 64

    @pl.loop(0, p_ref.shape[0])
    def _(q):
        @pl.loop(0, panel_rows, unroll=2)
        def _(w):
            k = q * panel_rows + w
            blocks = p_ref[q, pl.ds(pl.multiple_of(w * 64, 64), 64), :]
            sources, wanted = [], []
            for half in range(2):
                straight = blocks[:, half * 128:(half + 1) * 128]
                swapped = jnp.concatenate([straight[:, 64:], straight[:, :64]], axis=1)
                left = col_ref[k, 2 * half]
                right = col_ref[k, 2 * half + 1]
                sources += [straight.reshape(4, 16, 128), swapped.reshape(4, 16, 128)]
                wanted += [jnp.where(low, left, right - 1), jnp.where(low, right, left - 1)]
            for j in range(4):
                total = None
                for source, want in zip(sources, wanted):
                    term = source * jnp.where(want == 2 * j, 1.0, 0.0).astype(BF)[None]
                    total = term if total is None else total + term
                out_ref[k, j] = total.reshape(64, 128)

    out_ref[p_ref.shape[0] * panel_rows] = jnp.zeros(out_ref.shape[1:], BF)


def product_kernel(k_ref, *refs):
    a_refs, dense_ref, out_ref = refs[:-2], refs[-2], refs[-1]
    step = pl.program_id(0)
    sections = a_refs[0].shape[1]
    for u in range(6):
        i = step * 6 + u
        left, right = [], []
        for n, a_ref in enumerate(a_refs):
            for s in range(sections):
                left.append(a_ref[u, s])
                for slot in range(2):
                    k = k_ref[n, (i * sections + s) * 2 + slot]
                    right.append(jnp.concatenate([dense_ref[k, j] for j in range(4)], axis=1))
        total = jnp.dot(
            jnp.concatenate(left, axis=1), jnp.concatenate(right, axis=0), preferred_element_type=F32
        )
        for piece in range(4):
            row = u * 64 + piece * 16
            out_ref[row // 48, 0, row % 48:row % 48 + 16, :] = total[piece * 16:(piece + 1) * 16]


def split_kernel(c_ref, y_ref, *outs):
    for s, out in enumerate(outs):
        out[...] = y_ref[lax.rem(c_ref[0] + s, len(outs))].astype(BF)


def join_kernel(c_ref, *refs):
    pieces, out = refs[:-1], refs[-1]
    for s, piece in enumerate(pieces):
        width = piece.shape[1]
        source = lax.rem(c_ref[0] + len(pieces) - s, len(pieces))
        out[:, pl.ds(pl.multiple_of(source * width, width), width)] = piece[...]


VMEM_SPEC = pl.BlockSpec(memory_space=pltpu.VMEM)
SMEM_SPEC = pl.BlockSpec(memory_space=pltpu.SMEM)


def body(cols, a_vals, a_cols, a_count, panel_map, p_vals, p_cols, p_count):
    rows = a_vals.shape[0]
    sections = a_vals.shape[2]
    side = a_vals.shape[3]
    here = lax.axis_index("col")
    layer_map = lax.dynamic_index_in_dim(panel_map, lax.axis_index("layer"), 0, keepdims=False)
    panels = lax.dynamic_slice_in_dim(layer_map, here * sections, sections, 0)
    panel_rows = p_vals.shape[2]
    fine = panel_map.shape[1] * panel_rows

    slot_p = p_cols.shape[4]
    p_index = jnp.where(jnp.arange(slot_p) < p_count[0, 0, :, 0, None], p_cols[0, 0, :, 0], -9)
    p_flat = p_vals.reshape(panel_rows * side, slot_p * side)
    p_extra = jnp.pad(p_index.reshape(1, -1).astype(BF), ((0, 15), (0, slot_p * side - p_index.size)))
    p_all = lax.all_gather(jnp.concatenate([p_flat, p_extra], axis=0), "row", axis=0)
    p_col_all = p_all[:, panel_rows * side, :p_index.size].astype(jnp.int32).reshape(fine, slot_p)

    slot_a = a_cols.shape[3]
    k_index = jnp.where(
        jnp.arange(slot_a) < a_count[:, 0, :, None],
        panels[None, :, None] * panel_rows + a_cols[:, 0],
        fine,
    ).reshape(1, -1)
    mine = a_vals[:, 0]
    parts, indices = [mine], [k_index]
    for s in range(1, cols):
        to = [(n, (n + s) % cols) for n in range(cols)]
        indices.append(lax.ppermute(k_index, "col", to))
        parts.append(lax.ppermute(mine, "col", to))
    k_all = jnp.concatenate(indices, axis=0)

    dense = pl.pallas_call(
        expand_kernel,
        out_shape=jax.ShapeDtypeStruct((fine + 1, 4, side, 128), BF),
        in_specs=[SMEM_SPEC, VMEM_SPEC],
        out_specs=VMEM_SPEC,
        name="expand",
        cost_estimate=pl.CostEstimate(flops=0, bytes_accessed=6 << 20, transcendentals=0),
    )(p_col_all, p_all)

    width = CB * side
    groups = rows // 6
    partial_sum = pl.pallas_call(
        product_kernel,
        out_shape=jax.ShapeDtypeStruct((8, groups, 48, width), F32),
        grid_spec=pltpu.PrefetchScalarGridSpec(
            num_scalar_prefetch=1,
            grid=(groups,),
            in_specs=[pl.BlockSpec((6, sections, side, 128), lambda g, k: (g, 0, 0, 0))] * cols
            + [pl.BlockSpec((fine + 1, 4, side, 128), lambda g, k: (0, 0, 0, 0), pipeline_mode=pl.Buffered(1))],
            out_specs=pl.BlockSpec((8, 1, 48, width), lambda g, k: (0, g, 0, 0)),
        ),
        name="product",
        compiler_params=pltpu.CompilerParams(vmem_limit_bytes=48 << 20),
        cost_estimate=pl.CostEstimate(flops=2 * rows * side * 1024 * width, bytes_accessed=11 << 20, transcendentals=0),
    )(k_all, *parts, dense)

    mine_sum = lax.psum_scatter(partial_sum, "layer", scatter_dimension=0, tiled=True)[0]
    where = here.reshape(1)
    pieces = pl.pallas_call(
        split_kernel,
        out_shape=[jax.ShapeDtypeStruct((48, width), BF)] * cols,
        in_specs=[SMEM_SPEC, VMEM_SPEC],
        out_specs=[VMEM_SPEC] * cols,
        name="split",
    )(where, mine_sum)
    arrived = [pieces[0]]
    for s in range(1, cols):
        arrived.append(lax.ppermute(pieces[s], "col", [(n, (n + s) % cols) for n in range(cols)]))
    return pl.pallas_call(
        join_kernel,
        out_shape=jax.ShapeDtypeStruct((48, cols * width), BF),
        in_specs=[SMEM_SPEC] + [VMEM_SPEC] * cols,
        out_specs=VMEM_SPEC,
        name="join",
    )(where, *arrived)


def solution(mesh):
    placed = (
        P("row", "layer", "col", None, None),
        P("row", "layer", "col", None),
        P("row", "layer", "col"),
        P(),
        P("layer", "row", None, "col", None, None),
        P("layer", "row", None, "col", None),
        P("layer", "row", None, "col"),
    )
    return jax.shard_map(
        functools.partial(body, mesh.shape["col"]),
        mesh=mesh,
        in_specs=placed,
        out_specs=P(("row", "col", "layer"), None),
        check_vma=False,
    )
```

time: 457 us -> 139 us (0.30)
  waiting for transfers between devices: 307 us -> 82.2 us
  blocking collectives: 43.5 us -> 0 us
  local copies, waits for them, and re-layouts: 43.6 us -> 4.23 us
  other arithmetic: 26.6 us -> 4.02 us
  Pallas kernels: 0 us -> 20.1 us
  matrix products: 17.9 us -> 0 us
  starting transfers between devices: 0.08 us -> 14.2 us
    reduce_scatter x1, waiting for transfers between devices: 238 us -> 48.7 us  [body(): lax.psum_scatter(partial_sum, 'layer', scatter_dimension=0, tiled=True)[0]]
    all_gather x2 -> x1, waiting for transfers between devices: 68.7 us -> 0.02 us  [body(): lax.all_gather(jnp.concatenate([p_flat, p_extra], axis=0), 'row', axis=0)]
    all_gather x4 -> x0, blocking collectives: 43.5 us -> none  [the longest x1 12.2 us: body(): lax.all_gather(section_count, 'col', axis=3, tiled=True)]
    ppermute x0 -> x9, waiting for transfers between devices: none -> 33.4 us  [the longest x3 30.6 us: body(): indices.append(lax.ppermute(k_index, 'col', to))]
    select_n x3 -> x1, other arithmetic: 24 us -> 0.01 us  [body(): jnp.where(jnp.arange(slot_a) < a_count[:, 0, :, None], panels[None, :, No...]
    pallas_call x0 -> x4, Pallas kernels: none -> 20.1 us  [the longest x1 8.52 us: body(): pl.pallas_call(product_kernel, out_shape=jax.ShapeDtypeStruct((8, groups,...]
    dot_general x4 -> x0, matrix products: 17.9 us -> none  [the longest x2 12.8 us: accumulate(): jnp.einsum('ixk,ikn->ixn', masked, picked, preferred_element_type=jnp.flo...]
    reshape x4 -> x0, local copies, waits for them, and re-layouts: 17.7 us -> none  [the longest x2 12.5 us: expand(): dense_rows.astype(jnp.bfloat16)]
  transfers between devices with their start and end apart: 3 -> 11, of which waited for: 3 -> 6; matrix products, arithmetic and copies ran while one was open for 1% -> 3% of each run, Pallas kernels for 0% -> 6%
where the time goes in v1:
time: 139 us; the launch traced here: 138 us
  waiting for transfers between devices  82.2 us (59%)
  Pallas kernels  20.1 us (14%)
  starting transfers between devices  14.2 us (10%)
  between operations  13.5 us (10%)
  local copies, waits for them, and re-layouts  4.23 us (3%)
  other arithmetic  4.02 us (3%)
    reduce_scatter x1, waiting for transfers between devices, body(): lax.psum_scatter(partial_sum, 'layer', scatter_dimension=0, tiled=True)[0]  48.7 us
    ppermute x3, waiting for transfers between devices, body(): indices.append(lax.ppermute(k_index, 'col', to))  30.6 us
    pallas_call x1, Pallas kernels, body(): pl.pallas_call(product_kernel, out_shape=jax.ShapeDtypeStruct((8, groups,...  8.52 us
    pallas_call x1, Pallas kernels, body(): pl.pallas_call(expand_kernel, out_shape=jax.ShapeDtypeStruct((fine + 1, 4...  8.37 us
    ppermute x3, starting transfers between devices, body(): lax.ppermute(pieces[s], 'col', [(n, (n + s) % cols) for n in range(cols)])  5.72 us
    ppermute x3, starting transfers between devices, body(): parts.append(lax.ppermute(mine, 'col', to))  4.52 us
    ppermute x3, starting transfers between devices, body(): indices.append(lax.ppermute(k_index, 'col', to))  3.95 us
    ppermute x3, waiting for transfers between devices, body(): lax.ppermute(pieces[s], 'col', [(n, (n + s) % cols) for n in range(cols)])  2.82 us
  transfers between devices with their start and end apart: 11, of which 6 were waited for; matrix products, arithmetic and copies ran while one was open for 3% of the time, Pallas kernels for 6%

profile of v1, /device:TPU:8, one launch (start us, length us, event | category | flops | bytes accessed | tf_op | source)
XLA Modules:
  0.0 138.3 jit_solution(7470765675455416092)
XLA Ops:
  7.4 0.8 copy.13
  8.2 1.7 %fusion.1 = bf16[528,256]{1,0:T(8,128)(2,1)} fusion(bf16[1,32]{1,0:T(2,128)(2,1)S(1)} %select_convert_fusion, bf16[512,256]{1,0:T(8,128)(2,1)} %bitcast.22), kind=kLoop, calls=%fused_computation.2 | loop fusion | flops 811008 | bytes 532544 | tf_op jit(solution)/shard_map/concatenate | solution.py:96
  10.0 2.8 %collective-permute-start.5 = (bf16[24,2,64,128]{3,2,1,0:T(8,128)(2,1)}, bf16[24,2,64,128]{3,2,1,0:T(8,128)(2,1)S(1)}, u32[]{:S(2)}, u32[]{:S(2)}) collective-permute-start(bf16[24,2,64,128]{3,2,1,0:T(8,128)(2,1)} %bitcast.15), channel_id=1, source_target_pairs={{0,24},{8,0},{16,8},{24,16},{1,25},{9,1},{17,9},{25,17},{2,26},{10... | collective-permute-start | bytes 2359304 | tf_op jit(solution)/shard_map/ppermute | solution.py:110
  12.8 0.8 collective-permute-start.4
  13.6 0.9 collective-permute-start.3
  14.5 0.8 copy.11
  15.5 0.8 multiply_bitcast_fusion
  16.4 0.8 copy.12
  17.4 2.4 %collective-permute-start.2 = (s32[1,96]{1,0:T(1,128)S(1)}, s32[1,96]{1,0:T(1,128)S(1)}, u32[]{:S(2)}, u32[]{:S(2)}) collective-permute-start(s32[1,96]{1,0:T(1,128)S(1)} %add_select_fusion), channel_id=1, source_target_pairs={{0,24},{8,0},{16,8},{24,16},{1,25},{9,1},{17,9},{25,17},{2,26},{10... | collective-permute-start | bytes 1160 | tf_op jit(solution)/shard_map/ppermute | solution.py:109
  19.8 1.5 %collective-permute-start.1 = (s32[1,96]{1,0:T(1,128)S(1)}, s32[1,96]{1,0:T(1,128)S(1)}, u32[]{:S(2)}, u32[]{:S(2)}) collective-permute-start(s32[1,96]{1,0:T(1,128)S(1)} %add_select_fusion), channel_id=1, source_target_pairs={{0,16},{8,24},{16,0},{24,8},{1,17},{9,25},{17,1},{25,9},{2,18},{10... | collective-permute-start | bytes 1160 | tf_op jit(solution)/shard_map/ppermute | solution.py:109
  21.3 25.5 %collective-permute-done.2 = s32[1,96]{1,0:T(1,128)S(1)} collective-permute-done((s32[1,96]{1,0:T(1,128)S(1)}, s32[1,96]{1,0:T(1,128)S(1)}, u32[]{:S(2)}, u32[]{:S(2)}) %collective-permute-start.2) | collective-permute-done | bytes 416 | tf_op jit(solution)/shard_map/ppermute | solution.py:109
  46.8 3.6 %collective-permute-done.1 = s32[1,96]{1,0:T(1,128)S(1)} collective-permute-done((s32[1,96]{1,0:T(1,128)S(1)}, s32[1,96]{1,0:T(1,128)S(1)}, u32[]{:S(2)}, u32[]{:S(2)}) %collective-permute-start.1) | collective-permute-done | bytes 416 | tf_op jit(solution)/shard_map/ppermute | solution.py:109
  50.4 1.6 %collective-permute-done = s32[1,96]{1,0:T(1,128)S(1)} collective-permute-done((s32[1,96]{1,0:T(1,128)S(1)}, s32[1,96]{1,0:T(1,128)S(1)}, u32[]{:S(2)}, u32[]{:S(2)}) %collective-permute-start) | collective-permute-done | bytes 416 | tf_op jit(solution)/shard_map/ppermute | solution.py:109
  52.0 0.7 fusion.2
  53.4 8.4 %expand.1.refs_4_ = bf16[65,4,64,128]{3,2,1,0:T(8,128)(2,1)} custom-call(s32[64,4]{1,0:T(8,128)} %reshape.107.col_ref, bf16[8,528,256]{2,1,0:T(8,128)(2,1)} %bitcast.20), custom_call_target="tpu_custom_call" | custom-call | bytes 6291456 | tf_op jit(solution)/shard_map/expand/pallas_call | solution.py:113
  61.8 8.5 %product.1 = f32[8,4,48,512]{3,2,1,0:T(8,128)} custom-call(s32[4,96]{1,0:T(4,128)S(1)} %pad_add_fusion.k_ref, bf16[24,2,64,128]{3,2,1,0:T(8,128)(2,1)S(1)} %bitcast.18, bf16[24,2,64,128]{3,2,1,0:T(8,128)(2,1)S(1)} %collective-permute-done.3.refs_1_, bf16[24,2,64,128]{3,2,1,0:T(8,128)(2,1)S(1)} %collective-permute-done.4.refs_2_, ...), custom_call_target="tpu_custom_call" | custom-call | flops 1610612736 | bytes 11534336 | tf_op jit(solution)/shard_map/product/pallas_call | solution.py:124
  70.3 48.7 %reduce-scatter.2.cloned.1.call-done = f32[1,4,48,512]{3,2,1,0:T(8,128)} async-done(((f32[8,4,48,512]{3,2,1,0:T(8,128)}), f32[1,4,48,512]{3,2,1,0:T(8,128)}) %reduce-scatter.2.cloned.1.call-update) | async-done | bytes 393232 | tf_op jit(solution)/shard_map/reduce_scatter | solution.py:139
  119.1 1.7 %split.1 = (bf16[48,512]{1,0:T(8,128)(2,1)}, bf16[48,512]{1,0:T(8,128)(2,1)}, bf16[48,512]{1,0:T(8,128)(2,1)}, bf16[48,512]{1,0:T(8,128)(2,1)}) custom-call(s32[1]{0:T(128)} %bitcast.c_ref, f32[4,48,512]{2,1,0:T(8,128)} %bitcast.21), custom_call_target="tpu_custom_call" | custom-call | tf_op jit(solution)/shard_map/split/pallas_call | solution.py:141
  120.7 1.6 %collective-permute-start.6 = (bf16[48,512]{1,0:T(8,128)(2,1)}, bf16[48,512]{1,0:T(8,128)(2,1)S(1)}, u32[]{:S(2)}, u32[]{:S(2)}) collective-permute-start(bf16[48,512]{1,0:T(8,128)(2,1)} %get-tuple-element.10), channel_id=1, source_target_pairs={{0,8},{8,16},{16,24},{24,0},{1,9},{9,17},{17,25},{25,1},{2,10},{10... | collective-permute-start | bytes 147464 | tf_op jit(solution)/shard_map/ppermute | solution.py:150
  122.3 2.7 %collective-permute-start.7 = (bf16[48,512]{1,0:T(8,128)(2,1)}, bf16[48,512]{1,0:T(8,128)(2,1)S(1)}, u32[]{:S(2)}, u32[]{:S(2)}) collective-permute-start(bf16[48,512]{1,0:T(8,128)(2,1)} %get-tuple-element.11), channel_id=1, source_target_pairs={{0,16},{8,24},{16,0},{24,8},{1,17},{9,25},{17,1},{25,9},{2,18},{10... | collective-permute-start | bytes 147464 | tf_op jit(solution)/shard_map/ppermute | solution.py:150
  125.0 1.5 %collective-permute-start.8 = (bf16[48,512]{1,0:T(8,128)(2,1)}, bf16[48,512]{1,0:T(8,128)(2,1)S(1)}, u32[]{:S(2)}, u32[]{:S(2)}) collective-permute-start(bf16[48,512]{1,0:T(8,128)(2,1)} %get-tuple-element.12), channel_id=1, source_target_pairs={{0,24},{8,0},{16,8},{24,16},{1,25},{9,1},{17,9},{25,17},{2,26},{10... | collective-permute-start | bytes 147464 | tf_op jit(solution)/shard_map/ppermute | solution.py:150
  126.5 1.7 %collective-permute-done.7.refs_2_ = bf16[48,512]{1,0:T(8,128)(2,1)S(1)} collective-permute-done((bf16[48,512]{1,0:T(8,128)(2,1)}, bf16[48,512]{1,0:T(8,128)(2,1)S(1)}, u32[]{:S(2)}, u32[]{:S(2)}) %collective-permute-start.7) | collective-permute-done | bytes 49184 | tf_op jit(solution)/shard_map/ppermute | solution.py:150
  128.1 1.2 collective-permute-done.8.refs_3_
  129.9 1.6 %join.1 = bf16[48,2048]{1,0:T(8,128)(2,1)} custom-call(s32[1]{0:T(128)} %bitcast.c_ref, bf16[48,512]{1,0:T(8,128)(2,1)} %get-tuple-element.9.refs_0_, bf16[48,512]{1,0:T(8,128)(2,1)} %copy-done.1, bf16[48,512]{1,0:T(8,128)(2,1)} %copy-done.2, bf16[48,512]{1,0:T(8,128)(2,1)} %copy-done.3), custom_call_target="tpu_custom_call" | custom-call | tf_op jit(solution)/shard_map/join/pallas_call | solution.py:151
  (30 shorter events, 2.9 us)
Async XLA Ops:
  6.5 45.4 %all-gather.3.cloned.1.call-start = ((), (), s32[]{:S(2)}) async-start(), calls=%async_computation.2 | async-start | bytes 2433024 | tf_op jit(solution)/shard_map/all_gather | solution.py:96
  9.9 109.2 %reduce-scatter.2.cloned.1.call-start = ((), (), s32[]{:S(2)}) async-start(), calls=%async_computation.1 | async-start | bytes 3538944 | tf_op jit(solution)/shard_map/reduce_scatter | solution.py:139
  10.0 51.8 %collective-permute-start.5 = (bf16[24,2,64,128]{3,2,1,0:T(8,128)(2,1)}, bf16[24,2,64,128]{3,2,1,0:T(8,128)(2,1)S(1)}, u32[]{:S(2)}, u32[]{:S(2)}) collective-permute-start(bf16[24,2,64,128]{3,2,1,0:T(8,128)(2,1)} %bitcast.15), channel_id=1, source_target_pairs={{0,24},{8,0},{16,8},{24,16},{1,25},{9,1},{17,9},{25,17},{2,26},{10... | collective-permute-start | bytes 2359304 | tf_op jit(solution)/shard_map/ppermute | solution.py:110
  12.8 49.0 %collective-permute-start.4 = (bf16[24,2,64,128]{3,2,1,0:T(8,128)(2,1)}, bf16[24,2,64,128]{3,2,1,0:T(8,128)(2,1)S(1)}, u32[]{:S(2)}, u32[]{:S(2)}) collective-permute-start(bf16[24,2,64,128]{3,2,1,0:T(8,128)(2,1)} %bitcast.16), channel_id=1, source_target_pairs={{0,16},{8,24},{16,0},{24,8},{1,17},{9,25},{17,1},{25,9},{2,18},{10... | collective-permute-start | bytes 2359304 | tf_op jit(solution)/shard_map/ppermute | solution.py:110
  13.6 48.2 %collective-permute-start.3 = (bf16[24,2,64,128]{3,2,1,0:T(8,128)(2,1)}, bf16[24,2,64,128]{3,2,1,0:T(8,128)(2,1)S(1)}, u32[]{:S(2)}, u32[]{:S(2)}) collective-permute-start(bf16[24,2,64,128]{3,2,1,0:T(8,128)(2,1)} %bitcast.17), channel_id=1, source_target_pairs={{0,8},{8,16},{16,24},{24,0},{1,9},{9,17},{17,25},{25,1},{2,10},{10... | collective-permute-start | bytes 2359304 | tf_op jit(solution)/shard_map/ppermute | solution.py:110
  17.4 29.4 %collective-permute-start.2 = (s32[1,96]{1,0:T(1,128)S(1)}, s32[1,96]{1,0:T(1,128)S(1)}, u32[]{:S(2)}, u32[]{:S(2)}) collective-permute-start(s32[1,96]{1,0:T(1,128)S(1)} %add_select_fusion), channel_id=1, source_target_pairs={{0,24},{8,0},{16,8},{24,16},{1,25},{9,1},{17,9},{25,17},{2,26},{10... | collective-permute-start | bytes 1160 | tf_op jit(solution)/shard_map/ppermute | solution.py:109
  19.8 30.6 %collective-permute-start.1 = (s32[1,96]{1,0:T(1,128)S(1)}, s32[1,96]{1,0:T(1,128)S(1)}, u32[]{:S(2)}, u32[]{:S(2)}) collective-permute-start(s32[1,96]{1,0:T(1,128)S(1)} %add_select_fusion), channel_id=1, source_target_pairs={{0,16},{8,24},{16,0},{24,8},{1,17},{9,25},{17,1},{25,9},{2,18},{10... | collective-permute-start | bytes 1160 | tf_op jit(solution)/shard_map/ppermute | solution.py:109
  46.8 5.1 %collective-permute-start = (s32[1,96]{1,0:T(1,128)S(1)}, s32[1,96]{1,0:T(1,128)S(1)}, u32[]{:S(2)}, u32[]{:S(2)}) collective-permute-start(s32[1,96]{1,0:T(1,128)S(1)} %add_select_fusion), channel_id=1, source_target_pairs={{0,8},{8,16},{16,24},{24,0},{1,9},{9,17},{17,25},{25,1},{2,10},{10... | collective-permute-start | bytes 1160 | tf_op jit(solution)/shard_map/ppermute | solution.py:109
  53.4 8.4 %copy-start = (bf16[24,1,2,64,128]{4,3,2,1,0:T(8,128)(2,1)S(1)}, bf16[24,1,2,64,128]{4,3,2,1,0:T(8,128)(2,1)}, u32[]{:S(2)}) copy-start(bf16[24,1,2,64,128]{4,3,2,1,0:T(8,128)(2,1)} %param.7) | copy-start | bytes 2359300
  120.7 5.7 %collective-permute-start.6 = (bf16[48,512]{1,0:T(8,128)(2,1)}, bf16[48,512]{1,0:T(8,128)(2,1)S(1)}, u32[]{:S(2)}, u32[]{:S(2)}) collective-permute-start(bf16[48,512]{1,0:T(8,128)(2,1)} %get-tuple-element.10), channel_id=1, source_target_pairs={{0,8},{8,16},{16,24},{24,0},{1,9},{9,17},{17,25},{25,1},{2,10},{10... | collective-permute-start | bytes 147464 | tf_op jit(solution)/shard_map/ppermute | solution.py:150
  122.3 5.8 %collective-permute-start.7 = (bf16[48,512]{1,0:T(8,128)(2,1)}, bf16[48,512]{1,0:T(8,128)(2,1)S(1)}, u32[]{:S(2)}, u32[]{:S(2)}) collective-permute-start(bf16[48,512]{1,0:T(8,128)(2,1)} %get-tuple-element.11), channel_id=1, source_target_pairs={{0,16},{8,24},{16,0},{24,8},{1,17},{9,25},{17,1},{25,9},{2,18},{10... | collective-permute-start | bytes 147464 | tf_op jit(solution)/shard_map/ppermute | solution.py:150
  125.0 4.3 %collective-permute-start.8 = (bf16[48,512]{1,0:T(8,128)(2,1)}, bf16[48,512]{1,0:T(8,128)(2,1)S(1)}, u32[]{:S(2)}, u32[]{:S(2)}) collective-permute-start(bf16[48,512]{1,0:T(8,128)(2,1)} %get-tuple-element.12), channel_id=1, source_target_pairs={{0,24},{8,0},{16,8},{24,16},{1,25},{9,1},{17,9},{25,17},{2,26},{10... | collective-permute-start | bytes 147464 | tf_op jit(solution)/shard_map/ppermute | solution.py:150
  126.5 2.8 %copy-start.1 = (bf16[48,512]{1,0:T(8,128)(2,1)}, bf16[48,512]{1,0:T(8,128)(2,1)S(1)}, u32[]{:S(2)}) copy-start(bf16[48,512]{1,0:T(8,128)(2,1)S(1)} %collective-permute-done.6.refs_1_) | copy-start | bytes 147460
  128.1 1.2 copy-start.2
  129.3 0.6 copy-start.3
Sparse Core Ops, SparseCore 0:
  10.0 29.4 all-gather.2
  70.5 48.5 reduce-scatter.1

commit v2 on v1

v2 whole, which is shorter than its diff:
```python
import functools

import jax
import jax.numpy as jnp
from jax import lax
from jax.experimental import pallas as pl
from jax.experimental.pallas import tpu as pltpu
from jax.sharding import PartitionSpec as P

CB = 8
PANEL_ROWS = 8
BF = jnp.bfloat16
F32 = jnp.float32
VMEM_SPEC = pl.BlockSpec(memory_space=pltpu.VMEM)
SMEM_SPEC = pl.BlockSpec(memory_space=pltpu.SMEM)


def expand_kernel(core, row_ref, p_ref, *refs):
    out_ref = refs[-1]
    panels = out_ref.shape[0] // PANEL_ROWS
    row = row_ref[0]

    @pl.loop(0, p_ref.shape[0])
    def _(n):
        away = jnp.where(n == 0, 0, jnp.where(n == 1, panels - 2, jnp.where(n == 2, 2, 4)))
        panel = lax.rem(row + away, panels)
        if core:
            panel = panel + 1 - 2 * lax.rem(panel, 2)
        for w in range(PANEL_ROWS):
            blocks = p_ref[n, w * 64:(w + 1) * 64, :]
            sources, wanted = [], []
            for half in range(2):
                straight = blocks[:, half * 128:(half + 1) * 128]
                swapped = jnp.concatenate([straight[:, 64:], straight[:, :64]], axis=1)
                for side, source in enumerate((straight, swapped)):
                    sources.append(source.reshape(4, 16, 128))
                    r = PANEL_ROWS * 64 + 2 * w + half
                    want = p_ref[n, r:r + 1, side * 128:(side + 1) * 128]
                    wanted.append(jnp.broadcast_to(want.astype(F32), (16, 128)))
            for j in range(4):
                total = None
                for source, want in zip(sources, wanted):
                    term = source * jnp.where(want == 2.0 * j, 1.0, 0.0).astype(BF)[None]
                    total = term if total is None else total + term
                out_ref[panel * PANEL_ROWS + w, j] = total.reshape(64, 128)

    if core:
        out_ref[panels * PANEL_ROWS] = jnp.zeros(out_ref.shape[1:], BF)


def product_kernel(half, layers, here_ref, *refs):
    a_refs, k_far_ref, dense_ref = refs[:4], refs[4], refs[5]
    outs, (sums, k_vector, k_ref, sem) = refs[6:-4], refs[-4:]
    count = a_refs[0].shape[0] - 16
    for n in range(3):
        k_vector[n:n + 1] = a_refs[n][count:count + 1].astype(F32).astype(jnp.int32)
    k_vector[3:4] = k_far_ref[0:1].astype(F32).astype(jnp.int32)
    copy = pltpu.make_async_copy(k_vector, k_ref, sem)
    copy.start()
    copy.wait()
    sections = 2
    groups = sums.shape[1]
    for g in range(groups):
        @pl.loop(0, 2)
        def _(h):
            for v in range(3):
                u = h * 3 + v
                r = g * 6 + u
                i = half * groups * 6 + r
                left, right = [], []
                for n, a_ref in enumerate(a_refs):
                    for s in range(sections):
                        first = ((r if n == 3 else i) * sections + s) * 64
                        left.append(a_ref[pl.ds(pl.multiple_of(first, 64), 64), :])
                        for slot in range(2):
                            k = k_ref[n, (i * sections + s) * 2 + slot]
                            right.append(jnp.concatenate([dense_ref[k, j] for j in range(4)], axis=1))
                total = jnp.dot(
                    jnp.concatenate(left, axis=1), jnp.concatenate(right, axis=0), preferred_element_type=F32
                )
                for piece in range(4):
                    row = v * 64 + piece * 16
                    sums[h * 4 + row // 48, g, row % 48:row % 48 + 16, :] = total[piece * 16:(piece + 1) * 16]
    for o, out in enumerate(outs):
        out[...] = sums[lax.rem(here_ref[0] + o, layers)]


def split_kernel(c_ref, *refs):
    ins, outs, sums = refs[:6], refs[6:-1], refs[-1]
    for h in range(2):
        sums[2 * h:2 * h + 2] = ins[3 * h][...] + ins[3 * h + 1][...] + ins[3 * h + 2][...]
    for s, out in enumerate(outs):
        out[...] = sums[lax.rem(c_ref[0] + s, len(outs))].astype(BF)


def join_kernel(c_ref, *refs):
    pieces, out = refs[:-1], refs[-1]
    for s, piece in enumerate(pieces):
        width = piece.shape[1]
        source = lax.rem(c_ref[0] + len(pieces) - s, len(pieces))
        out[:, pl.ds(pl.multiple_of(source * width, width), width)] = piece[...]


def shift(x, axis, size, by):
    return lax.ppermute(x, axis, [(n, (n + by) % size) for n in range(size)])


def body(a_vals, a_cols, a_count, panel_map, p_vals, p_cols, p_count):
    rows = a_vals.shape[0]
    sections = a_vals.shape[2]
    side = a_vals.shape[3]
    cols, layers, grid_rows = 4, 8, 8
    here = lax.axis_index("col")
    layer = lax.axis_index("layer")
    row = lax.axis_index("row")
    layer_map = lax.dynamic_index_in_dim(panel_map, layer, 0, keepdims=False)
    panels = lax.dynamic_slice_in_dim(layer_map, here * sections, sections, 0)
    panel_rows = p_vals.shape[2]
    fine = panel_map.shape[1] * panel_rows

    slot_a = a_cols.shape[3]
    k_index = jnp.where(
        jnp.arange(slot_a) < a_count[:, 0, :, None],
        panels[None, :, None] * panel_rows + a_cols[:, 0],
        fine,
    ).reshape(1, -1)
    k_tile = jnp.pad(k_index.astype(BF), ((0, 15), (0, 2 * side - k_index.size)))
    own = jnp.concatenate([a_vals[:, 0].reshape(rows * sections * side, 2 * side), k_tile], axis=0)
    from_left, from_right = shift(own, "col", cols, 1), shift(own, "col", cols, -1)

    slot_p = p_cols.shape[4]
    index = jnp.where(jnp.arange(slot_p) < p_count[0, 0, :, 0, None], p_cols[0, 0, :, 0], -9)
    odd = index.reshape(panel_rows, 2, 2)
    odd = jnp.concatenate([odd - jnp.array([0, 1]), odd[:, :, ::-1] - jnp.array([0, 1])], axis=2)
    wanted = jnp.broadcast_to(odd[:, :, :, None].astype(BF), (panel_rows, 2, 4, side))
    mine = jnp.concatenate(
        [p_vals.reshape(panel_rows * side, slot_p * side), wanted.reshape(2 * panel_rows, 4 * side)], axis=0
    )
    p_line = [shift(mine, "row", grid_rows, by) for by in (2, -2, 4)]
    p_line, from_left, from_right = lax.optimization_barrier((p_line, from_left, from_right))
    p_line = jnp.stack([mine] + p_line)
    p_pair = lax.ppermute(p_line, "row", [(n, n ^ 1) for n in range(grid_rows)])

    cut = rows * sections * side // 2
    far_first = shift(from_left[:cut], "col", cols, 1)
    far_second = shift(from_right[cut:], "col", cols, -1)
    far = [far_first, far_second[:cut]]
    k_far = far_second[cut:]

    dense = []
    for core, part in enumerate((p_line, p_pair)):
        dense = [pl.pallas_call(
            functools.partial(expand_kernel, core),
            out_shape=jax.ShapeDtypeStruct((fine + 1, 4, side, 128), BF),
            in_specs=[SMEM_SPEC] + [VMEM_SPEC] * (1 + core),
            out_specs=VMEM_SPEC,
            input_output_aliases={2: 0} if core else {},
            name="expand",
            compiler_params=pltpu.CompilerParams(vmem_limit_bytes=14 << 20),
            cost_estimate=pl.CostEstimate(flops=0, bytes_accessed=10 << 20, transcendentals=0),
        )(row.reshape(1), part, *dense)]
    dense = dense[0]

    width = CB * side
    groups = rows // 12
    block = (groups, 48, width)
    finals = []
    for half in range(2):
        part = pl.pallas_call(
            functools.partial(product_kernel, half, layers),
            out_shape=[jax.ShapeDtypeStruct(block, F32)] * layers,
            in_specs=[SMEM_SPEC] + [VMEM_SPEC] * 6,
            out_specs=[VMEM_SPEC] * layers,
            scratch_shapes=[
                pltpu.VMEM((layers,) + block, F32),
                pltpu.VMEM((8, 128), jnp.int32),
                pltpu.SMEM((8, 128), jnp.int32),
                pltpu.SemaphoreType.DMA(()),
            ],
            name="product",
            compiler_params=pltpu.CompilerParams(vmem_limit_bytes=16 << 20),
            cost_estimate=pl.CostEstimate(flops=rows * side * 1024 * width, bytes_accessed=8 << 20, transcendentals=0),
        )(layer.reshape(1), own, from_left, from_right, far[half], k_far, dense)
        reach = 4 if half == 0 else 3
        up, down = part[reach], part[reach + 1]
        for step in range(4):
            if step < reach:
                up = shift(up, "layer", layers, 1)
                if step < reach - 1:
                    up = up + part[reach - 1 - step]
            if step < 7 - reach:
                down = shift(down, "layer", layers, -1)
                if step < 6 - reach:
                    down = down + part[reach + 2 + step]
        finals += [part[0], up, down]

    where = here.reshape(1)
    pieces = pl.pallas_call(
        split_kernel,
        out_shape=[jax.ShapeDtypeStruct((48, width), BF)] * cols,
        in_specs=[SMEM_SPEC] + [VMEM_SPEC] * 6,
        out_specs=[VMEM_SPEC] * cols,
        scratch_shapes=[pltpu.VMEM((cols, 48, width), F32)],
        name="split",
        compiler_params=pltpu.CompilerParams(vmem_limit_bytes=4 << 20),
    )(where, *finals)
    arrived = [pieces[0]] + [shift(pieces[s], "col", cols, s) for s in range(1, cols)]
    return pl.pallas_call(
        join_kernel,
        out_shape=jax.ShapeDtypeStruct((48, cols * width), BF),
        in_specs=[SMEM_SPEC] + [VMEM_SPEC] * cols,
        out_specs=VMEM_SPEC,
        name="join",
        compiler_params=pltpu.CompilerParams(vmem_limit_bytes=2 << 20),
    )(where, *arrived)


def solution(mesh):
    placed = (
        P("row", "layer", "col", None, None),
        P("row", "layer", "col", None),
        P("row", "layer", "col"),
        P(),
        P("layer", "row", None, "col", None, None),
        P("layer", "row", None, "col", None),
        P("layer", "row", None, "col"),
    )
    return jax.shard_map(
        body,
        mesh=mesh,
        in_specs=placed,
        out_specs=P(("row", "col", "layer"), None),
        check_vma=False,
    )
```

time: 139 us -> 101 us (0.73)
  waiting for transfers between devices: 82.2 us -> 41.6 us
  starting transfers between devices: 14.2 us -> 37.4 us
  between operations: 13.5 us -> 0.24 us
  Pallas kernels: 20.1 us -> 13.1 us
    reduce_scatter x1 -> x0, waiting for transfers between devices: 48.7 us -> none  [body(): lax.psum_scatter(partial_sum, 'layer', scatter_dimension=0, tiled=True)[0]]
    ppermute x9 -> x25, starting transfers between devices: 14.2 us -> 37.4 us  [the longest x24 37.3 us: shift(): return lax.ppermute(x, axis, [(n, (n + by) % size) for n in range(size)])]
    ppermute x9 -> x25, waiting for transfers between devices: 33.4 us -> 41.6 us  [the longest x24 41.5 us: shift(): return lax.ppermute(x, axis, [(n, (n + by) % size) for n in range(size)])]
    pallas_call x2 -> x4, Pallas kernels: 16.9 us -> 12.3 us  [the longest x2 7.76 us: body(): pl.pallas_call(functools.partial(product_kernel, half, layers), out_shape...]
    slice x0 -> x4, local copies, waits for them, and re-layouts: none -> 3.27 us  [the longest x1 1.02 us: body(): far = [far_first, far_second[:cut]]]
    pallas_call x1, Pallas kernels: 1.68 us -> 0.08 us  [body(): pl.pallas_call(split_kernel, out_shape=[jax.ShapeDtypeStruct((48, width),...]
  transfers between devices with their start and end apart: 11 -> 25, of which waited for: 6 -> 16; matrix products, arithmetic and copies ran while one was open for 3% -> 4% of each run, Pallas kernels for 6% -> 12%
where the time goes in v2:
time: 101 us; the launch traced here: 100 us
  waiting for transfers between devices  41.6 us (41%)
  starting transfers between devices  37.4 us (37%)
  Pallas kernels  13.1 us (13%)
  local copies, waits for them, and re-layouts  5.58 us (6%)
  other arithmetic  2.65 us (3%)
    ppermute x24, waiting for transfers between devices, shift(): return lax.ppermute(x, axis, [(n, (n + by) % size) for n in range(size)])  41.5 us
    ppermute x24, starting transfers between devices, shift(): return lax.ppermute(x, axis, [(n, (n + by) % size) for n in range(size)])  37.3 us
    pallas_call x2, Pallas kernels, body(): pl.pallas_call(functools.partial(product_kernel, half, layers), out_shape...  7.76 us
    pallas_call x2, Pallas kernels, body(): pl.pallas_call(functools.partial(expand_kernel, core), out_shape=jax.Shap...  4.53 us
  transfers between devices with their start and end apart: 25, of which 16 were waited for; matrix products, arithmetic and copies ran while one was open for 4% of the time, Pallas kernels for 12%

profile of v2, /device:TPU:8, one launch (start us, length us, event | category | flops | bytes accessed | tf_op | source)
XLA Modules:
  0.0 100.5 jit_solution(14959528032272678378)
XLA Ops:
  4.1 1.6 %collective-permute-start.3 = (bf16[3088,128]{1,0:T(8,128)(2,1)S(1)}, bf16[3088,128]{1,0:T(8,128)(2,1)S(1)}, u32[]{:S(2)}, u32[]{:S(2)}) collective-permute-start(bf16[3088,128]{1,0:T(8,128)(2,1)S(1)} %fusion.1.refs_0_), channel_id=1, source_target_pairs={{0,8},{8,16},{16,24},{24,0},{1,9},{9,17},{17,25},{25,1},{2,10},{10... | collective-permute-start | bytes 2371592 | tf_op jit(solution)/shard_map/ppermute | solution.py:105
  5.7 1.7 %collective-permute-start.4 = (bf16[3088,128]{1,0:T(8,128)(2,1)S(1)}, bf16[3088,128]{1,0:T(8,128)(2,1)S(1)}, u32[]{:S(2)}, u32[]{:S(2)}) collective-permute-start(bf16[3088,128]{1,0:T(8,128)(2,1)S(1)} %fusion.1.refs_0_), channel_id=1, source_target_pairs={{0,24},{8,0},{16,8},{24,16},{1,25},{9,1},{17,9},{25,17},{2,26},{10... | collective-permute-start | bytes 2371592 | tf_op jit(solution)/shard_map/ppermute | solution.py:105
  7.9 1.7 %collective-permute-start = (bf16[528,256]{1,0:T(8,128)(2,1)S(1)}, bf16[528,256]{1,0:T(8,128)(2,1)S(1)}, u32[]{:S(2)}, u32[]{:S(2)}) collective-permute-start(bf16[528,256]{1,0:T(8,128)(2,1)S(1)} %get-tuple-element.58), channel_id=1, source_target_pairs={{0,64},{32,96},{64,128},{96,160},{128,192},{160,224},{192,0},{224,... | collective-permute-start | bytes 811016 | tf_op jit(solution)/shard_map/ppermute | solution.py:105
  10.3 2.1 %collective-permute-start.2 = (bf16[528,256]{1,0:T(8,128)(2,1)S(1)}, bf16[528,256]{1,0:T(8,128)(2,1)S(1)}, u32[]{:S(2)}, u32[]{:S(2)}) collective-permute-start(bf16[528,256]{1,0:T(8,128)(2,1)S(1)} %get-tuple-element.58), channel_id=1, source_target_pairs={{0,128},{32,160},{64,192},{96,224},{128,0},{160,32},{192,64},{224,... | collective-permute-start | bytes 811016 | tf_op jit(solution)/shard_map/ppermute | solution.py:105
  12.3 5.2 %collective-permute-done = bf16[528,256]{1,0:T(8,128)(2,1)S(1)} collective-permute-done((bf16[528,256]{1,0:T(8,128)(2,1)S(1)}, bf16[528,256]{1,0:T(8,128)(2,1)S(1)}, u32[]{:S(2)}, u32[]{:S(2)}) %collective-permute-start) | collective-permute-done | bytes 270368 | tf_op jit(solution)/shard_map/ppermute | solution.py:105
  18.3 5.2 %collective-permute-done.2 = bf16[528,256]{1,0:T(8,128)(2,1)S(1)} collective-permute-done((bf16[528,256]{1,0:T(8,128)(2,1)S(1)}, bf16[528,256]{1,0:T(8,128)(2,1)S(1)}, u32[]{:S(2)}, u32[]{:S(2)}) %collective-permute-start.2) | collective-permute-done | bytes 270368 | tf_op jit(solution)/shard_map/ppermute | solution.py:105
  25.8 3.0 %collective-permute-start.6 = (bf16[1552,128]{1,0:T(8,128)(2,1)}, bf16[1552,128]{1,0:T(8,128)(2,1)}, u32[]{:S(2)}, u32[]{:S(2)}) collective-permute-start(bf16[1552,128]{1,0:T(8,128)(2,1)} %slice.13), channel_id=1, source_target_pairs={{0,24},{8,0},{16,8},{24,16},{1,25},{9,1},{17,9},{25,17},{2,26},{10... | collective-permute-start | bytes 1191944 | tf_op jit(solution)/shard_map/ppermute | solution.py:105
  29.6 1.6 %expand.2.refs_0_ = bf16[65,4,64,128]{3,2,1,0:T(8,128)(2,1)S(1)} custom-call(s32[1]{0:T(128)} %bitcast.8.row_ref, bf16[4,528,256]{2,1,0:T(8,128)(2,1)S(1)} %pad_maximum_fusion.p_ref), custom_call_target="tpu_custom_call" | custom-call | bytes 10485760 | tf_op jit(solution)/shard_map/expand/pallas_call | solution.py:152
  31.2 7.0 %collective-permute-done.6 = bf16[1552,128]{1,0:T(8,128)(2,1)} collective-permute-done((bf16[1552,128]{1,0:T(8,128)(2,1)}, bf16[1552,128]{1,0:T(8,128)(2,1)}, u32[]{:S(2)}, u32[]{:S(2)}) %collective-permute-start.6) | collective-permute-done | bytes 397344 | tf_op jit(solution)/shard_map/ppermute | solution.py:105
  39.9 2.9 %expand.3.refs_5_ = bf16[65,4,64,128]{3,2,1,0:T(8,128)(2,1)S(1)} custom-call(s32[1]{0:T(128)} %bitcast.8.row_ref, bf16[4,528,256]{2,1,0:T(8,128)(2,1)} %collective-permute-done.7.p_ref, bf16[65,4,64,128]{3,2,1,0:T(8,128)(2,1)S(1)} %expand.2.refs_0_), custom_call_target="tpu_custom_call", output_to_operand_aliasing={{}: (2, {})} | custom-call | bytes 10485760 | tf_op jit(solution)/shard_map/expand/pallas_call | solution.py:152
  42.8 3.4 %product.3 = (f32[2,48,512]{2,1,0:T(8,128)S(1)}, f32[2,48,512]{2,1,0:T(8,128)S(1)}, f32[2,48,512]{2,1,0:T(8,128)S(1)}, f32[2,48,512]{2,1,0:T(8,128)S(1)}, f32[2,...) custom-call(s32[1]{0:T(128)} %bitcast.1.here_ref, ...), custom_call_target="tpu_custom_call" | custom-call | flops 805306368 | bytes 8388608 | tf_op jit(solution)/shard_map/product/pallas_call | solution.py:169
  46.3 5.9 %collective-permute-start.18 = (f32[2,48,512]{2,1,0:T(8,128)S(1)}, f32[2,48,512]{2,1,0:T(8,128)S(1)}, u32[]{:S(2)}, u32[]{:S(2)}) collective-permute-start(f32[2,48,512]{2,1,0:T(8,128)S(1)} %get-tuple-element.47), channel_id=1, source_target_pairs={{0,7},{1,0},{2,1},{3,2},{4,3},{5,4},{6,5},{7,6},{8,15},{9,8},{10,9... | collective-permute-start | bytes 589832 | tf_op jit(solution)/shard_map/ppermute | solution.py:105
  52.2 4.3 %product.2 = (f32[2,48,512]{2,1,0:T(8,128)S(1)}, f32[2,48,512]{2,1,0:T(8,128)S(1)}, f32[2,48,512]{2,1,0:T(8,128)S(1)}, f32[2,48,512]{2,1,0:T(8,128)S(1)}, f32[2,...) custom-call(s32[1]{0:T(128)} %bitcast.1.here_ref, ...), custom_call_target="tpu_custom_call" | custom-call | flops 805306368 | bytes 8388608 | tf_op jit(solution)/shard_map/product/pallas_call | solution.py:169
  56.7 3.2 %collective-permute-start.12 = (f32[2,48,512]{2,1,0:T(8,128)S(1)}, f32[2,48,512]{2,1,0:T(8,128)S(1)}, u32[]{:S(2)}, u32[]{:S(2)}) collective-permute-start(f32[2,48,512]{2,1,0:T(8,128)S(1)} %get-tuple-element.40), channel_id=1, source_target_pairs={{0,7},{1,0},{2,1},{3,2},{4,3},{5,4},{6,5},{7,6},{8,15},{9,8},{10,9... | collective-permute-start | bytes 589832 | tf_op jit(solution)/shard_map/ppermute | solution.py:105
  60.0 2.0 %collective-permute-start.19 = (f32[2,48,512]{2,1,0:T(8,128)S(1)}, f32[2,48,512]{2,1,0:T(8,128)S(1)}, u32[]{:S(2)}, u32[]{:S(2)}) collective-permute-start(f32[2,48,512]{2,1,0:T(8,128)S(1)} %add.75), channel_id=1, source_target_pairs={{0,7},{1,0},{2,1},{3,2},{4,3},{5,4},{6,5},{7,6},{8,15},{9,8},{10,9... | collective-permute-start | bytes 589832 | tf_op jit(solution)/shard_map/ppermute | solution.py:105
  62.0 3.7 %collective-permute-done.8 = f32[2,48,512]{2,1,0:T(8,128)S(1)} collective-permute-done((f32[2,48,512]{2,1,0:T(8,128)S(1)}, f32[2,48,512]{2,1,0:T(8,128)S(1)}, u32[]{:S(2)}, u32[]{:S(2)}) %collective-permute-start.8) | collective-permute-done | bytes 196640 | tf_op jit(solution)/shard_map/ppermute | solution.py:105
  65.8 4.1 %collective-permute-done.15 = f32[2,48,512]{2,1,0:T(8,128)S(1)} collective-permute-done((f32[2,48,512]{2,1,0:T(8,128)S(1)}, f32[2,48,512]{2,1,0:T(8,128)S(1)}, u32[]{:S(2)}, u32[]{:S(2)}) %collective-permute-start.15) | collective-permute-done | bytes 196640 | tf_op jit(solution)/shard_map/ppermute | solution.py:105
  70.0 3.3 %collective-permute-start.13 = (f32[2,48,512]{2,1,0:T(8,128)S(1)}, f32[2,48,512]{2,1,0:T(8,128)S(1)}, u32[]{:S(2)}, u32[]{:S(2)}) collective-permute-start(f32[2,48,512]{2,1,0:T(8,128)S(1)} %add.71), channel_id=1, source_target_pairs={{0,7},{1,0},{2,1},{3,2},{4,3},{5,4},{6,5},{7,6},{8,15},{9,8},{10,9... | collective-permute-start | bytes 589832 | tf_op jit(solution)/shard_map/ppermute | solution.py:105
  75.6 3.5 %collective-permute-done.16 = f32[2,48,512]{2,1,0:T(8,128)S(1)} collective-permute-done((f32[2,48,512]{2,1,0:T(8,128)S(1)}, f32[2,48,512]{2,1,0:T(8,128)S(1)}, u32[]{:S(2)}, u32[]{:S(2)}) %collective-permute-start.16) | collective-permute-done | bytes 196640 | tf_op jit(solution)/shard_map/ppermute | solution.py:105
  79.2 3.3 %collective-permute-start.14 = (f32[2,48,512]{2,1,0:T(8,128)S(1)}, f32[2,48,512]{2,1,0:T(8,128)S(1)}, u32[]{:S(2)}, u32[]{:S(2)}) collective-permute-start(f32[2,48,512]{2,1,0:T(8,128)S(1)} %add.72), channel_id=1, source_target_pairs={{0,7},{1,0},{2,1},{3,2},{4,3},{5,4},{6,5},{7,6},{8,15},{9,8},{10,9... | collective-permute-start | bytes 589832 | tf_op jit(solution)/shard_map/ppermute | solution.py:105
  84.7 2.7 %collective-permute-done.17.refs_4_ = f32[2,48,512]{2,1,0:T(8,128)S(1)} collective-permute-done((f32[2,48,512]{2,1,0:T(8,128)S(1)}, f32[2,48,512]{2,1,0:T(8,128)S(1)}, u32[]{:S(2)}, u32[]{:S(2)}) %collective-permute-start.17) | collective-permute-done | bytes 196640 | tf_op jit(solution)/shard_map/ppermute | solution.py:105
  88.3 2.1 %collective-permute-done.11.refs_1_ = f32[2,48,512]{2,1,0:T(8,128)S(1)} collective-permute-done((f32[2,48,512]{2,1,0:T(8,128)S(1)}, f32[2,48,512]{2,1,0:T(8,128)S(1)}, u32[]{:S(2)}, u32[]{:S(2)}) %collective-permute-start.11) | collective-permute-done | bytes 196640 | tf_op jit(solution)/shard_map/ppermute | solution.py:105
  91.6 4.2 %collective-permute-start.23 = (bf16[48,512]{1,0:T(8,128)(2,1)S(1)}, bf16[48,512]{1,0:T(8,128)(2,1)S(1)}, u32[]{:S(2)}, u32[]{:S(2)}) collective-permute-start(bf16[48,512]{1,0:T(8,128)(2,1)S(1)} %get-tuple-element.53), channel_id=1, source_target_pairs={{0,16},{8,24},{16,0},{24,8},{1,17},{9,25},{17,1},{25,9},{2,18},{10... | collective-permute-start | bytes 147464 | tf_op jit(solution)/shard_map/ppermute | solution.py:105
  96.3 2.0 %collective-permute-done.23.refs_2_ = bf16[48,512]{1,0:T(8,128)(2,1)S(1)} collective-permute-done((bf16[48,512]{1,0:T(8,128)(2,1)S(1)}, bf16[48,512]{1,0:T(8,128)(2,1)S(1)}, u32[]{:S(2)}, u32[]{:S(2)}) %collective-permute-start.23) | collective-permute-done | bytes 49184 | tf_op jit(solution)/shard_map/ppermute | solution.py:105
  (72 shorter events, 20.7 us)
Async XLA Ops:
  4.1 20.7 %collective-permute-start.3 = (bf16[3088,128]{1,0:T(8,128)(2,1)S(1)}, bf16[3088,128]{1,0:T(8,128)(2,1)S(1)}, u32[]{:S(2)}, u32[]{:S(2)}) collective-permute-start(bf16[3088,128]{1,0:T(8,128)(2,1)S(1)} %fusion.1.refs_0_), channel_id=1, source_target_pairs={{0,8},{8,16},{16,24},{24,0},{1,9},{9,17},{17,25},{25,1},{2,10},{10... | collective-permute-start | bytes 2371592 | tf_op jit(solution)/shard_map/ppermute | solution.py:105
  5.7 19.1 %collective-permute-start.4 = (bf16[3088,128]{1,0:T(8,128)(2,1)S(1)}, bf16[3088,128]{1,0:T(8,128)(2,1)S(1)}, u32[]{:S(2)}, u32[]{:S(2)}) collective-permute-start(bf16[3088,128]{1,0:T(8,128)(2,1)S(1)} %fusion.1.refs_0_), channel_id=1, source_target_pairs={{0,24},{8,0},{16,8},{24,16},{1,25},{9,1},{17,9},{25,17},{2,26},{10... | collective-permute-start | bytes 2371592 | tf_op jit(solution)/shard_map/ppermute | solution.py:105
  7.9 9.6 %collective-permute-start = (bf16[528,256]{1,0:T(8,128)(2,1)S(1)}, bf16[528,256]{1,0:T(8,128)(2,1)S(1)}, u32[]{:S(2)}, u32[]{:S(2)}) collective-permute-start(bf16[528,256]{1,0:T(8,128)(2,1)S(1)} %get-tuple-element.58), channel_id=1, source_target_pairs={{0,64},{32,96},{64,128},{96,160},{128,192},{160,224},{192,0},{224,... | collective-permute-start | bytes 811016 | tf_op jit(solution)/shard_map/ppermute | solution.py:105
  9.6 8.7 %collective-permute-start.1 = (bf16[528,256]{1,0:T(8,128)(2,1)S(1)}, bf16[528,256]{1,0:T(8,128)(2,1)S(1)}, u32[]{:S(2)}, u32[]{:S(2)}) collective-permute-start(bf16[528,256]{1,0:T(8,128)(2,1)S(1)} %get-tuple-element.58), channel_id=1, source_target_pairs={{0,192},{32,224},{64,0},{96,32},{128,64},{160,96},{192,128},{224,1... | collective-permute-start | bytes 811016 | tf_op jit(solution)/shard_map/ppermute | solution.py:105
  10.3 13.2 %collective-permute-start.2 = (bf16[528,256]{1,0:T(8,128)(2,1)S(1)}, bf16[528,256]{1,0:T(8,128)(2,1)S(1)}, u32[]{:S(2)}, u32[]{:S(2)}) collective-permute-start(bf16[528,256]{1,0:T(8,128)(2,1)S(1)} %get-tuple-element.58), channel_id=1, source_target_pairs={{0,128},{32,160},{64,192},{96,224},{128,0},{160,32},{192,64},{224,... | collective-permute-start | bytes 811016 | tf_op jit(solution)/shard_map/ppermute | solution.py:105
  24.9 15.0 %collective-permute-start.7 = (bf16[4,528,256]{2,1,0:T(8,128)(2,1)S(1)}, bf16[4,528,256]{2,1,0:T(8,128)(2,1)}, u32[]{:S(2)}, u32[]{:S(2)}) collective-permute-start(bf16[4,528,256]{2,1,0:T(8,128)(2,1)S(1)} %pad_maximum_fusion.p_ref), channel_id=1, source_target_pairs={{0,32},{32,0},{64,96},{96,64},{128,160},{160,128},{192,224},{224,1... | collective-permute-start | bytes 3244040 | tf_op jit(solution)/shard_map/ppermute | solution.py:142
  25.8 12.4 %collective-permute-start.6 = (bf16[1552,128]{1,0:T(8,128)(2,1)}, bf16[1552,128]{1,0:T(8,128)(2,1)}, u32[]{:S(2)}, u32[]{:S(2)}) collective-permute-start(bf16[1552,128]{1,0:T(8,128)(2,1)} %slice.13), channel_id=1, source_target_pairs={{0,24},{8,0},{16,8},{24,16},{1,25},{9,1},{17,9},{25,17},{2,26},{10... | collective-permute-start | bytes 1191944 | tf_op jit(solution)/shard_map/ppermute | solution.py:105
  29.6 22.6 %collective-permute-start.5 = (bf16[1536,128]{1,0:T(8,128)(2,1)}, bf16[1536,128]{1,0:T(8,128)(2,1)}, u32[]{:S(2)}, u32[]{:S(2)}) collective-permute-start(bf16[1536,128]{1,0:T(8,128)(2,1)} %slice.12), channel_id=1, source_target_pairs={{0,8},{8,16},{16,24},{24,0},{1,9},{9,17},{17,25},{25,1},{2,10},{10... | collective-permute-start | bytes 1179656 | tf_op jit(solution)/shard_map/ppermute | solution.py:105
  46.3 13.7 %collective-permute-start.18 = (f32[2,48,512]{2,1,0:T(8,128)S(1)}, f32[2,48,512]{2,1,0:T(8,128)S(1)}, u32[]{:S(2)}, u32[]{:S(2)}) collective-permute-start(f32[2,48,512]{2,1,0:T(8,128)S(1)} %get-tuple-element.47), channel_id=1, source_target_pairs={{0,7},{1,0},{2,1},{3,2},{4,3},{5,4},{6,5},{7,6},{8,15},{9,8},{10,9... | collective-permute-start | bytes 589832 | tf_op jit(solution)/shard_map/ppermute | solution.py:105
  56.5 9.1 %collective-permute-start.8 = (f32[2,48,512]{2,1,0:T(8,128)S(1)}, f32[2,48,512]{2,1,0:T(8,128)S(1)}, u32[]{:S(2)}, u32[]{:S(2)}) collective-permute-start(f32[2,48,512]{2,1,0:T(8,128)S(1)} %get-tuple-element.36), channel_id=1, source_target_pairs={{0,1},{1,2},{2,3},{3,4},{4,5},{5,6},{6,7},{7,0},{8,9},{9,10},{10,1... | collective-permute-start | bytes 589832 | tf_op jit(solution)/shard_map/ppermute | solution.py:105
  56.6 13.2 %collective-permute-start.15 = (f32[2,48,512]{2,1,0:T(8,128)S(1)}, f32[2,48,512]{2,1,0:T(8,128)S(1)}, u32[]{:S(2)}, u32[]{:S(2)}) collective-permute-start(f32[2,48,512]{2,1,0:T(8,128)S(1)} %get-tuple-element.44), channel_id=1, source_target_pairs={{0,1},{1,2},{2,3},{3,4},{4,5},{5,6},{6,7},{7,0},{8,9},{9,10},{10,1... | collective-permute-start | bytes 589832 | tf_op jit(solution)/shard_map/ppermute | solution.py:105
  56.7 13.3 %collective-permute-start.12 = (f32[2,48,512]{2,1,0:T(8,128)S(1)}, f32[2,48,512]{2,1,0:T(8,128)S(1)}, u32[]{:S(2)}, u32[]{:S(2)}) collective-permute-start(f32[2,48,512]{2,1,0:T(8,128)S(1)} %get-tuple-element.40), channel_id=1, source_target_pairs={{0,7},{1,0},{2,1},{3,2},{4,3},{5,4},{6,5},{7,6},{8,15},{9,8},{10,9... | collective-permute-start | bytes 589832 | tf_op jit(solution)/shard_map/ppermute | solution.py:105
  60.0 13.4 %collective-permute-start.19 = (f32[2,48,512]{2,1,0:T(8,128)S(1)}, f32[2,48,512]{2,1,0:T(8,128)S(1)}, u32[]{:S(2)}, u32[]{:S(2)}) collective-permute-start(f32[2,48,512]{2,1,0:T(8,128)S(1)} %add.75), channel_id=1, source_target_pairs={{0,7},{1,0},{2,1},{3,2},{4,3},{5,4},{6,5},{7,6},{8,15},{9,8},{10,9... | collective-permute-start | bytes 589832 | tf_op jit(solution)/shard_map/ppermute | solution.py:105
  65.7 8.7 %collective-permute-start.9 = (f32[2,48,512]{2,1,0:T(8,128)S(1)}, f32[2,48,512]{2,1,0:T(8,128)S(1)}, u32[]{:S(2)}, u32[]{:S(2)}) collective-permute-start(f32[2,48,512]{2,1,0:T(8,128)S(1)} %add.68), channel_id=1, source_target_pairs={{0,1},{1,2},{2,3},{3,4},{4,5},{5,6},{6,7},{7,0},{8,9},{9,10},{10,1... | collective-permute-start | bytes 589832 | tf_op jit(solution)/shard_map/ppermute | solution.py:105
  69.9 9.1 %collective-permute-start.16 = (f32[2,48,512]{2,1,0:T(8,128)S(1)}, f32[2,48,512]{2,1,0:T(8,128)S(1)}, u32[]{:S(2)}, u32[]{:S(2)}) collective-permute-start(f32[2,48,512]{2,1,0:T(8,128)S(1)} %add.73), channel_id=1, source_target_pairs={{0,1},{1,2},{2,3},{3,4},{4,5},{5,6},{6,7},{7,0},{8,9},{9,10},{10,1... | collective-permute-start | bytes 589832 | tf_op jit(solution)/shard_map/ppermute | solution.py:105
  70.0 9.1 %collective-permute-start.13 = (f32[2,48,512]{2,1,0:T(8,128)S(1)}, f32[2,48,512]{2,1,0:T(8,128)S(1)}, u32[]{:S(2)}, u32[]{:S(2)}) collective-permute-start(f32[2,48,512]{2,1,0:T(8,128)S(1)} %add.71), channel_id=1, source_target_pairs={{0,7},{1,0},{2,1},{3,2},{4,3},{5,4},{6,5},{7,6},{8,15},{9,8},{10,9... | collective-permute-start | bytes 589832 | tf_op jit(solution)/shard_map/ppermute | solution.py:105
  73.4 9.1 %collective-permute-start.20 = (f32[2,48,512]{2,1,0:T(8,128)S(1)}, f32[2,48,512]{2,1,0:T(8,128)S(1)}, u32[]{:S(2)}, u32[]{:S(2)}) collective-permute-start(f32[2,48,512]{2,1,0:T(8,128)S(1)} %add.76), channel_id=1, source_target_pairs={{0,7},{1,0},{2,1},{3,2},{4,3},{5,4},{6,5},{7,6},{8,15},{9,8},{10,9... | collective-permute-start | bytes 589832 | tf_op jit(solution)/shard_map/ppermute | solution.py:105
  74.5 8.9 %collective-permute-start.10 = (f32[2,48,512]{2,1,0:T(8,128)S(1)}, f32[2,48,512]{2,1,0:T(8,128)S(1)}, u32[]{:S(2)}, u32[]{:S(2)}) collective-permute-start(f32[2,48,512]{2,1,0:T(8,128)S(1)} %add.69), channel_id=1, source_target_pairs={{0,1},{1,2},{2,3},{3,4},{4,5},{5,6},{6,7},{7,0},{8,9},{9,10},{10,1... | collective-permute-start | bytes 589832 | tf_op jit(solution)/shard_map/ppermute | solution.py:105
  79.1 8.3 %collective-permute-start.17 = (f32[2,48,512]{2,1,0:T(8,128)S(1)}, f32[2,48,512]{2,1,0:T(8,128)S(1)}, u32[]{:S(2)}, u32[]{:S(2)}) collective-permute-start(f32[2,48,512]{2,1,0:T(8,128)S(1)} %add.74), channel_id=1, source_target_pairs={{0,1},{1,2},{2,3},{3,4},{4,5},{5,6},{6,7},{7,0},{8,9},{9,10},{10,1... | collective-permute-start | bytes 589832 | tf_op jit(solution)/shard_map/ppermute | solution.py:105
  79.2 8.2 %collective-permute-start.14 = (f32[2,48,512]{2,1,0:T(8,128)S(1)}, f32[2,48,512]{2,1,0:T(8,128)S(1)}, u32[]{:S(2)}, u32[]{:S(2)}) collective-permute-start(f32[2,48,512]{2,1,0:T(8,128)S(1)} %add.72), channel_id=1, source_target_pairs={{0,7},{1,0},{2,1},{3,2},{4,3},{5,4},{6,5},{7,6},{8,15},{9,8},{10,9... | collective-permute-start | bytes 589832 | tf_op jit(solution)/shard_map/ppermute | solution.py:105
  82.5 5.7 %collective-permute-start.21 = (f32[2,48,512]{2,1,0:T(8,128)S(1)}, f32[2,48,512]{2,1,0:T(8,128)S(1)}, u32[]{:S(2)}, u32[]{:S(2)}) collective-permute-start(f32[2,48,512]{2,1,0:T(8,128)S(1)} %add.77), channel_id=1, source_target_pairs={{0,7},{1,0},{2,1},{3,2},{4,3},{5,4},{6,5},{7,6},{8,15},{9,8},{10,9... | collective-permute-start | bytes 589832 | tf_op jit(solution)/shard_map/ppermute | solution.py:105
  83.4 7.0 %collective-permute-start.11 = (f32[2,48,512]{2,1,0:T(8,128)S(1)}, f32[2,48,512]{2,1,0:T(8,128)S(1)}, u32[]{:S(2)}, u32[]{:S(2)}) collective-permute-start(f32[2,48,512]{2,1,0:T(8,128)S(1)} %add.70), channel_id=1, source_target_pairs={{0,1},{1,2},{2,3},{3,4},{4,5},{5,6},{6,7},{7,0},{8,9},{9,10},{10,1... | collective-permute-start | bytes 589832 | tf_op jit(solution)/shard_map/ppermute | solution.py:105
  90.5 5.9 %collective-permute-start.22 = (bf16[48,512]{1,0:T(8,128)(2,1)S(1)}, bf16[48,512]{1,0:T(8,128)(2,1)S(1)}, u32[]{:S(2)}, u32[]{:S(2)}) collective-permute-start(bf16[48,512]{1,0:T(8,128)(2,1)S(1)} %get-tuple-element.52), channel_id=1, source_target_pairs={{0,8},{8,16},{16,24},{24,0},{1,9},{9,17},{17,25},{25,1},{2,10},{10... | collective-permute-start | bytes 147464 | tf_op jit(solution)/shard_map/ppermute | solution.py:105
  91.6 6.8 %collective-permute-start.23 = (bf16[48,512]{1,0:T(8,128)(2,1)S(1)}, bf16[48,512]{1,0:T(8,128)(2,1)S(1)}, u32[]{:S(2)}, u32[]{:S(2)}) collective-permute-start(bf16[48,512]{1,0:T(8,128)(2,1)S(1)} %get-tuple-element.53), channel_id=1, source_target_pairs={{0,16},{8,24},{16,0},{24,8},{1,17},{9,25},{17,1},{25,9},{2,18},{10... | collective-permute-start | bytes 147464 | tf_op jit(solution)/shard_map/ppermute | solution.py:105
  (4 other events, 26.9 us)

commit v3 on v2

v3 whole, which is shorter than its diff:
```python
import functools

import jax
import jax.numpy as jnp
from jax import lax
from jax.experimental import pallas as pl
from jax.experimental.pallas import tpu as pltpu
from jax.sharding import PartitionSpec as P

CB = 8
PANEL_ROWS = 8
BF = jnp.bfloat16
F32 = jnp.float32
VMEM_SPEC = pl.BlockSpec(memory_space=pltpu.VMEM)
SMEM_SPEC = pl.BlockSpec(memory_space=pltpu.SMEM)


def expand_kernel(core, row_ref, p_ref, *refs):
    out_ref = refs[-1]
    panels = out_ref.shape[0] // PANEL_ROWS
    row = row_ref[0]

    @pl.loop(0, p_ref.shape[0])
    def _(n):
        panel = row ^ (2 * n + core)
        for w in range(PANEL_ROWS):
            blocks = p_ref[n, w * 64:(w + 1) * 64, :]
            sources, wanted = [], []
            for half in range(2):
                straight = blocks[:, half * 128:(half + 1) * 128]
                swapped = jnp.concatenate([straight[:, 64:], straight[:, :64]], axis=1)
                for side, source in enumerate((straight, swapped)):
                    sources.append(source.reshape(4, 16, 128))
                    r = PANEL_ROWS * 64 + 2 * w + half
                    want = p_ref[n, r:r + 1, side * 128:(side + 1) * 128]
                    wanted.append(jnp.broadcast_to(want.astype(F32), (16, 128)))
            for j in range(4):
                total = None
                for source, want in zip(sources, wanted):
                    term = source * jnp.where(want == 2.0 * j, 1.0, 0.0).astype(BF)[None]
                    total = term if total is None else total + term
                out_ref[panel * PANEL_ROWS + w, j] = total.reshape(64, 128)

    if core:
        out_ref[panels * PANEL_ROWS] = jnp.zeros(out_ref.shape[1:], BF)


def multiply(sums, add, k_ref, dense_ref, lefts):
    for g in range(sums.shape[1]):
        @pl.loop(0, 2)
        def _(h):
            for v in range(3):
                i = g * 6 + h * 3 + v
                left, right = [], []
                for n, (a_ref, base) in enumerate(lefts(g)):
                    for s in range(2):
                        first = ((i - base) * 2 + s) * 64
                        left.append(a_ref[pl.ds(pl.multiple_of(first, 64), 64), :])
                        for slot in range(2):
                            k = k_ref[n, (i * 2 + s) * 2 + slot]
                            right.append(jnp.concatenate([dense_ref[k, j] for j in range(4)], axis=1))
                total = jnp.dot(
                    jnp.concatenate(left, axis=1), jnp.concatenate(right, axis=0), preferred_element_type=F32
                )
                for piece in range(4):
                    row = v * 64 + piece * 16
                    where = (h * 4 + row // 48, g, slice(row % 48, row % 48 + 16))
                    term = total[piece * 16:(piece + 1) * 16]
                    sums[where] = sums[where] + term if add else term


def load_k(k_rows, k_vector, k_ref, sem):
    for n, k in enumerate(k_rows):
        k_vector[n:n + 1] = k.astype(F32).astype(jnp.int32)
    copy = pltpu.make_async_copy(k_vector, k_ref, sem)
    copy.start()
    copy.wait()


def near_kernel(*refs):
    a_refs, dense_ref, sums, scratch = refs[:3], refs[3], refs[4], refs[5:]
    count = a_refs[0].shape[0] - 16
    load_k([a[count:count + 1] for a in a_refs], *scratch)
    multiply(sums, False, scratch[1], dense_ref, lambda g: [(a, 0) for a in a_refs])


def code(x_of, out, scales):
    scales[...] = jnp.zeros_like(scales)
    for g in range(12):
        x = x_of(g)
        most = jnp.maximum(jnp.max(jnp.abs(x), axis=0, keepdims=True), 1e-33)
        e = jnp.ceil(64.0 * (jnp.log2(most) - 15.0)) + 1.0
        scales[g:g + 1] = e
        out[g * 16:(g + 1) * 16] = jnp.floor(x * jnp.exp2(e * (-1.0 / 64)) + 0.5).astype(jnp.int32).astype(jnp.int16)
    out[192:208] = scales[...].astype(jnp.int32).astype(jnp.int16)


def decoded(ref, scales):
    scales[...] = jnp.exp2(ref[192:208].astype(jnp.int32).astype(F32) * (1.0 / 64))
    return lambda g: ref[g * 16:(g + 1) * 16].astype(jnp.int32).astype(F32) * scales[g:g + 1]


def rows_of(sums, index):
    return lambda g: sums[index, g // 3, (g % 3) * 16:(g % 3) * 16 + 16, :]


def far_kernel(layer_ref, sums_in, first_ref, second_ref, dense_ref, sums, up, down, *scratch):
    count = second_ref.shape[0] - 16
    k_scratch, scales = scratch[:3], scratch[3]
    load_k([second_ref[count:count + 1]], *k_scratch)
    half = sums.shape[1] // 2
    multiply(
        sums, True, k_scratch[1], dense_ref,
        lambda g: [(first_ref, 0) if g < half else (second_ref, 6 * half)],
    )
    layers = sums.shape[0]
    code(rows_of(sums, lax.rem(layer_ref[0] + 4, layers)), up, scales)
    code(rows_of(sums, lax.rem(layer_ref[0] + 5, layers)), down, scales)


def hop_kernel(offset, layer_ref, arrived, sums, out, scales_in, scales):
    mine = rows_of(sums, lax.rem(layer_ref[0] + offset, sums.shape[0]))
    other = decoded(arrived, scales_in)
    code(lambda g: mine(g) + other(g), out, scales)


def split_kernel(here_ref, layer_ref, up, down, sums, *refs):
    outs, (whole, scales_up, scales_down) = refs[:-3], refs[-3:]
    mine = rows_of(sums, layer_ref[0])
    above, below = decoded(up, scales_up), decoded(down, scales_down)
    for g in range(12):
        whole[g // 3, (g % 3) * 16:(g % 3) * 16 + 16] = mine(g) + above(g) + below(g)
    for s, out in enumerate(outs):
        out[...] = whole[here_ref[0] ^ s].astype(BF)


def join_kernel(c_ref, *refs):
    pieces, out = refs[:-1], refs[-1]
    for s, piece in enumerate(pieces):
        width = piece.shape[1]
        source = c_ref[0] ^ s
        out[:, pl.ds(pl.multiple_of(source * width, width), width)] = piece[...]


def swap(x, axis, size, mask):
    return lax.ppermute(x, axis, [(n, n ^ mask) for n in range(size)])


def shift(x, axis, size, by):
    return lax.ppermute(x, axis, [(n, (n + by) % size) for n in range(size)])


def body(a_vals, a_cols, a_count, panel_map, p_vals, p_cols, p_count):
    rows = a_vals.shape[0]
    sections = a_vals.shape[2]
    side = a_vals.shape[3]
    cols, layers, grid_rows = 4, 8, 8
    here = lax.axis_index("col")
    layer = lax.axis_index("layer")
    row = lax.axis_index("row")
    layer_map = lax.dynamic_index_in_dim(panel_map, layer, 0, keepdims=False)
    panels = lax.dynamic_slice_in_dim(layer_map, here * sections, sections, 0)
    panel_rows = p_vals.shape[2]
    fine = panel_map.shape[1] * panel_rows

    slot_a = a_cols.shape[3]
    k_index = jnp.where(
        jnp.arange(slot_a) < a_count[:, 0, :, None],
        panels[None, :, None] * panel_rows + a_cols[:, 0],
        fine,
    ).reshape(1, -1)
    k_tile = jnp.pad(k_index.astype(BF), ((0, 15), (0, 2 * side - k_index.size)))
    own = jnp.concatenate([a_vals[:, 0].reshape(rows * sections * side, 2 * side), k_tile], axis=0)
    from_left, from_right = swap(own, "col", cols, 1), swap(own, "col", cols, 3)

    slot_p = p_cols.shape[4]
    index = jnp.where(jnp.arange(slot_p) < p_count[0, 0, :, 0, None], p_cols[0, 0, :, 0], -9)
    odd = index.reshape(panel_rows, 2, 2)
    odd = jnp.concatenate([odd - jnp.array([0, 1]), odd[:, :, ::-1] - jnp.array([0, 1])], axis=2)
    wanted = jnp.broadcast_to(odd[:, :, :, None].astype(BF), (panel_rows, 2, 4, side))
    mine = jnp.concatenate(
        [p_vals.reshape(panel_rows * side, slot_p * side), wanted.reshape(2 * panel_rows, 4 * side)], axis=0
    )
    p_line = [swap(mine, "row", grid_rows, mask) for mask in (2, 4, 6)]
    p_line, from_left, from_right = lax.optimization_barrier((p_line, from_left, from_right))
    p_line = jnp.stack([mine] + p_line)
    p_pair = swap(p_line, "row", grid_rows, 1)

    cut = rows * sections * side // 2
    far_first = swap(from_right[:cut], "col", cols, 1)
    far_second = swap(from_left[cut:], "col", cols, 3)

    dense = []
    for core, part in enumerate((p_line, p_pair)):
        dense = [pl.pallas_call(
            functools.partial(expand_kernel, core),
            out_shape=jax.ShapeDtypeStruct((fine + 1, 4, side, 128), BF),
            in_specs=[SMEM_SPEC] + [VMEM_SPEC] * (1 + core),
            out_specs=VMEM_SPEC,
            input_output_aliases={2: 0} if core else {},
            name="expand",
            compiler_params=pltpu.CompilerParams(vmem_limit_bytes=14 << 20),
            cost_estimate=pl.CostEstimate(flops=0, bytes_accessed=10 << 20, transcendentals=0),
        )(row.reshape(1), part, *dense)]
    dense = dense[0]

    width = CB * side
    sums_shape = jax.ShapeDtypeStruct((layers, rows // 6, 48, width), F32)
    coded = jax.ShapeDtypeStruct((208, width), jnp.int16)
    k_scratch = [pltpu.VMEM((8, 128), jnp.int32), pltpu.SMEM((8, 128), jnp.int32), pltpu.SemaphoreType.DMA(())]
    scales = pltpu.VMEM((16, width), F32)
    layer = layer.reshape(1)
    sums = pl.pallas_call(
        near_kernel,
        out_shape=sums_shape,
        in_specs=[VMEM_SPEC] * 4,
        out_specs=VMEM_SPEC,
        scratch_shapes=k_scratch,
        name="near",
        compiler_params=pltpu.CompilerParams(vmem_limit_bytes=14 << 20),
        cost_estimate=pl.CostEstimate(flops=4 << 30, bytes_accessed=11 << 20, transcendentals=0),
    )(own, from_left, from_right, dense)
    sums, up, down = pl.pallas_call(
        far_kernel,
        out_shape=[sums_shape, coded, coded],
        in_specs=[SMEM_SPEC] + [VMEM_SPEC] * 4,
        out_specs=[VMEM_SPEC] * 3,
        scratch_shapes=k_scratch + [scales],
        input_output_aliases={1: 0},
        name="far",
        compiler_params=pltpu.CompilerParams(vmem_limit_bytes=14 << 20),
        cost_estimate=pl.CostEstimate(flops=1 << 30, bytes_accessed=9 << 20, transcendentals=0),
    )(layer, sums, far_first, far_second, dense)

    def hop(offset, arrived):
        return pl.pallas_call(
            functools.partial(hop_kernel, offset),
            out_shape=coded,
            in_specs=[SMEM_SPEC] + [VMEM_SPEC] * 2,
            out_specs=VMEM_SPEC,
            scratch_shapes=[scales, scales],
            name="hop",
            compiler_params=pltpu.CompilerParams(vmem_limit_bytes=4 << 20),
            cost_estimate=pl.CostEstimate(flops=0, bytes_accessed=1 << 20, transcendentals=0),
        )(layer, arrived, sums)

    for step in range(4):
        up = shift(up, "layer", layers, 1)
        if step < 3:
            up = hop(3 - step, up)
            down = shift(down, "layer", layers, -1)
        if step < 2:
            down = hop(6 + step, down)

    where = here.reshape(1)
    pieces = pl.pallas_call(
        split_kernel,
        out_shape=[jax.ShapeDtypeStruct((48, width), BF)] * cols,
        in_specs=[SMEM_SPEC] * 2 + [VMEM_SPEC] * 3,
        out_specs=[VMEM_SPEC] * cols,
        scratch_shapes=[pltpu.VMEM((cols, 48, width), F32), scales, scales],
        name="split",
        compiler_params=pltpu.CompilerParams(vmem_limit_bytes=4 << 20),
    )(where, layer, up, down, sums)
    arrived = [pieces[0]] + [swap(pieces[s], "col", cols, s) for s in range(1, cols)]
    return pl.pallas_call(
        join_kernel,
        out_shape=jax.ShapeDtypeStruct((48, cols * width), BF),
        in_specs=[SMEM_SPEC] + [VMEM_SPEC] * cols,
        out_specs=VMEM_SPEC,
        name="join",
        compiler_params=pltpu.CompilerParams(vmem_limit_bytes=2 << 20),
    )(where, *arrived)


def solution(mesh):
    placed = (
        P("row", "layer", "col", None, None),
        P("row", "layer", "col", None),
        P("row", "layer", "col"),
        P(),
        P("layer", "row", None, "col", None, None),
        P("layer", "row", None, "col", None),
        P("layer", "row", None, "col"),
    )
    return jax.shard_map(
        body,
        mesh=mesh,
        in_specs=placed,
        out_specs=P(("row", "col", "layer"), None),
        check_vma=False,
    )
```

time: 101 us -> 88.7 us (0.88)
  starting transfers between devices: 37.4 us -> 27.4 us
  local copies, waits for them, and re-layouts: 5.58 us -> 3.36 us
    ppermute x24 -> x7, starting transfers between devices: 37.3 us -> 13 us  [shift(): return lax.ppermute(x, axis, [(n, (n + by) % size) for n in range(size)])]
    ppermute x1 -> x11, waiting for transfers between devices: 0.01 us -> 22.4 us  [swap(): return lax.ppermute(x, axis, [(n, n ^ mask) for n in range(size)])]
    ppermute x24 -> x7, waiting for transfers between devices: 41.5 us -> 19.2 us  [shift(): return lax.ppermute(x, axis, [(n, (n + by) % size) for n in range(size)])]
    ppermute x1 -> x11, starting transfers between devices: 0.09 us -> 14.4 us  [swap(): return lax.ppermute(x, axis, [(n, n ^ mask) for n in range(size)])]
    slice x4 -> x2, local copies, waits for them, and re-layouts: 3.27 us -> 0.06 us  [the longest x1 0.03 us: body(): far_second = swap(from_left[cut:], 'col', cols, 3)]
    pallas_call x2 -> x7, Pallas kernels: 7.76 us -> 9.38 us  [the longest x1 4.93 us: body(): pl.pallas_call(near_kernel, out_shape=sums_shape, in_specs=[VMEM_SPEC] *...]
    pallas_call x2, Pallas kernels: 4.53 us -> 3.3 us  [body(): pl.pallas_call(functools.partial(expand_kernel, core), out_shape=jax.Shap...]
  transfers between devices with their start and end apart: 25 -> 18, of which waited for: 16 -> 12; matrix products, arithmetic and copies ran while one was open for 4% -> 1% of each run, Pallas kernels for 12% -> 11%
where the time goes in v3:
time: 88.7 us; the launch traced here: 88.5 us
  waiting for transfers between devices  41.6 us (47%)
  starting transfers between devices  27.4 us (31%)
  Pallas kernels  13.5 us (15%)
  local copies, waits for them, and re-layouts  3.36 us (4%)
  other arithmetic  2.33 us (3%)
    ppermute x11, waiting for transfers between devices, swap(): return lax.ppermute(x, axis, [(n, n ^ mask) for n in range(size)])  22.4 us
    ppermute x7, waiting for transfers between devices, shift(): return lax.ppermute(x, axis, [(n, (n + by) % size) for n in range(size)])  19.2 us
    ppermute x11, starting transfers between devices, swap(): return lax.ppermute(x, axis, [(n, n ^ mask) for n in range(size)])  14.4 us
    ppermute x7, starting transfers between devices, shift(): return lax.ppermute(x, axis, [(n, (n + by) % size) for n in range(size)])  13 us
    pallas_call x1, Pallas kernels, body(): pl.pallas_call(near_kernel, out_shape=sums_shape, in_specs=[VMEM_SPEC] *...  4.93 us
    pallas_call x2, Pallas kernels, body(): pl.pallas_call(functools.partial(expand_kernel, core), out_shape=jax.Shap...  3.3 us
    pallas_call x1, Pallas kernels, body(): pl.pallas_call(far_kernel, out_shape=[sums_shape, coded, coded], in_specs...  3.13 us
  transfers between devices with their start and end apart: 18, of which 12 were waited for; matrix products, arithmetic and copies ran while one was open for 1% of the time, Pallas kernels for 11%

profile of v3, /device:TPU:8, one launch (start us, length us, event | category | flops | bytes accessed | tf_op | source)
XLA Modules:
  0.0 88.5 jit_solution(14226601120872193688)
XLA Ops:
  4.1 1.6 %collective-permute-start.3 = (bf16[3088,128]{1,0:T(8,128)(2,1)S(1)}, bf16[3088,128]{1,0:T(8,128)(2,1)S(1)}, u32[]{:S(2)}, u32[]{:S(2)}) collective-permute-start(bf16[3088,128]{1,0:T(8,128)(2,1)S(1)} %fusion.1.refs_0_), channel_id=1, source_target_pairs={{0,8},{8,0},{16,24},{24,16},{1,9},{9,1},{17,25},{25,17},{2,10},{10... | collective-permute-start | bytes 2371592 | tf_op jit(solution)/shard_map/ppermute | solution.py:146
  5.7 2.1 %collective-permute-start.4 = (bf16[3088,128]{1,0:T(8,128)(2,1)S(1)}, bf16[3088,128]{1,0:T(8,128)(2,1)S(1)}, u32[]{:S(2)}, u32[]{:S(2)}) collective-permute-start(bf16[3088,128]{1,0:T(8,128)(2,1)S(1)} %fusion.1.refs_0_), channel_id=1, source_target_pairs={{0,24},{8,16},{16,8},{24,0},{1,25},{9,17},{17,9},{25,1},{2,26},{10... | collective-permute-start | bytes 2371592 | tf_op jit(solution)/shard_map/ppermute | solution.py:146
  8.8 2.6 %collective-permute-start.1 = (bf16[528,256]{1,0:T(8,128)(2,1)S(1)}, bf16[528,256]{1,0:T(8,128)(2,1)S(1)}, u32[]{:S(2)}, u32[]{:S(2)}) collective-permute-start(bf16[528,256]{1,0:T(8,128)(2,1)S(1)} %get-tuple-element.32), channel_id=1, source_target_pairs={{0,128},{32,160},{64,192},{96,224},{128,0},{160,32},{192,64},{224,... | collective-permute-start | bytes 811016 | tf_op jit(solution)/shard_map/ppermute | solution.py:146
  11.9 5.9 %collective-permute-done = bf16[528,256]{1,0:T(8,128)(2,1)S(1)} collective-permute-done((bf16[528,256]{1,0:T(8,128)(2,1)S(1)}, bf16[528,256]{1,0:T(8,128)(2,1)S(1)}, u32[]{:S(2)}, u32[]{:S(2)}) %collective-permute-start) | collective-permute-done | bytes 270368 | tf_op jit(solution)/shard_map/ppermute | solution.py:146
  17.8 5.2 %collective-permute-done.1 = bf16[528,256]{1,0:T(8,128)(2,1)S(1)} collective-permute-done((bf16[528,256]{1,0:T(8,128)(2,1)S(1)}, bf16[528,256]{1,0:T(8,128)(2,1)S(1)}, u32[]{:S(2)}, u32[]{:S(2)}) %collective-permute-start.1) | collective-permute-done | bytes 270368 | tf_op jit(solution)/shard_map/ppermute | solution.py:146
  24.3 1.7 %collective-permute-done.4.refs_2_ = bf16[3088,128]{1,0:T(8,128)(2,1)S(1)} collective-permute-done((bf16[3088,128]{1,0:T(8,128)(2,1)S(1)}, bf16[3088,128]{1,0:T(8,128)(2,1)S(1)}, u32[]{:S(2)}, u32[]{:S(2)}) %collective-permute-start.4) | collective-permute-done | bytes 790560 | tf_op jit(solution)/shard_map/ppermute | solution.py:146
  27.2 1.6 %expand.2.refs_0_ = bf16[65,4,64,128]{3,2,1,0:T(8,128)(2,1)S(1)} custom-call(s32[1]{0:T(128)} %bitcast.8.row_ref, bf16[4,528,256]{2,1,0:T(8,128)(2,1)S(1)} %pad_maximum_fusion.p_ref), custom_call_target="tpu_custom_call" | custom-call | bytes 10485760 | tf_op jit(solution)/shard_map/expand/pallas_call | solution.py:195
  29.1 2.2 %collective-permute-start.7 = (bf16[1552,128]{1,0:T(8,128)(2,1)S(1)}, bf16[1552,128]{1,0:T(8,128)(2,1)S(1)}, u32[]{:S(2)}, u32[]{:S(2)}) collective-permute-start(bf16[1552,128]{1,0:T(8,128)(2,1)S(1)} %slice.7), channel_id=1, source_target_pairs={{0,24},{8,16},{16,8},{24,0},{1,25},{9,17},{17,9},{25,1},{2,26},{10... | collective-permute-start | bytes 1191944 | tf_op jit(solution)/shard_map/ppermute | solution.py:146
  31.3 1.7 %expand.3.refs_3_.dense_ref = bf16[65,4,64,128]{3,2,1,0:T(8,128)(2,1)S(1)} custom-call(s32[1]{0:T(128)} %bitcast.8.row_ref, bf16[4,528,256]{2,1,0:T(8,128)(2,1)S(1)} %collective-permute-done.5.p_ref, bf16[65,4,64,128]{3,2,1,0:T(8,128)(2,1)S(1)} %expand.2.refs_0_), custom_call_target="tpu_custom_call", output_to_operand_aliasing={{}: (2, {})} | custom-call | bytes 10485760 | tf_op jit(solution)/shard_map/expand/pallas_call | solution.py:195
  32.9 4.9 %near.1.sums_in = f32[8,4,48,512]{3,2,1,0:T(8,128)S(1)} custom-call(bf16[3088,128]{1,0:T(8,128)(2,1)S(1)} %fusion.1.refs_0_, bf16[3088,128]{1,0:T(8,128)(2,1)S(1)} %copy-done.1, bf16[3088,128]{1,0:T(8,128)(2,1)S(1)} %copy-done.3, bf16[65,4,64,128]{3,2,1,0:T(8,128)(2,1)S(1)} %expand.3.refs_3_.dense_ref), custom_call_target="tpu_custom_call" | custom-call | flops 4294967296 | bytes 11534336 | tf_op jit(solution)/shard_map/near/pallas_call | solution.py:213
  37.9 2.6 %collective-permute-done.6.first_ref = bf16[1536,128]{1,0:T(8,128)(2,1)S(1)} collective-permute-done((bf16[1536,128]{1,0:T(8,128)(2,1)S(1)}, bf16[1536,128]{1,0:T(8,128)(2,1)S(1)}, u32[]{:S(2)}, u32[]{:S(2)}) %collective-permute-start.6) | collective-permute-done | bytes 393248 | tf_op jit(solution)/shard_map/ppermute | solution.py:146
  40.5 1.4 %collective-permute-done.7.second_ref = bf16[1552,128]{1,0:T(8,128)(2,1)S(1)} collective-permute-done((bf16[1552,128]{1,0:T(8,128)(2,1)S(1)}, bf16[1552,128]{1,0:T(8,128)(2,1)S(1)}, u32[]{:S(2)}, u32[]{:S(2)}) %collective-permute-start.7) | collective-permute-done | bytes 397344 | tf_op jit(solution)/shard_map/ppermute | solution.py:146
  42.0 3.1 %far.1 = (f32[8,4,48,512]{3,2,1,0:T(8,128)S(1)}, s16[208,512]{1,0:T(8,128)(2,1)S(1)}, s16[208,512]{1,0:T(8,128)(2,1)S(1)}) custom-call(s32[1]{0:T(128)} %bitcast.1.layer_ref, f32[8,4,48,512]{3,2,1,0:T(8,128)S(1)} %near.1.sums_in, bf16[1536,128]{1,0:T(8,128)(2,1)S(1)} %collective-permute-done.6.first_ref, ...), custom_call_target="tpu_custom_call", output_to_operand_aliasing={{0}: (1, {})} | custom-call | flops 1073741824 | bytes 9437184 | tf_op jit(solution)/shard_map/far/pallas_call | solution.py:223
  45.1 2.0 %collective-permute-start.8 = (s16[208,512]{1,0:T(8,128)(2,1)S(1)}, s16[208,512]{1,0:T(8,128)(2,1)S(1)}, u32[]{:S(2)}, u32[]{:S(2)}) collective-permute-start(s16[208,512]{1,0:T(8,128)(2,1)S(1)} %get-tuple-element.22), channel_id=1, source_target_pairs={{0,1},{1,2},{2,3},{3,4},{4,5},{5,6},{6,7},{7,0},{8,9},{9,10},{10,1... | collective-permute-start | bytes 638984 | tf_op jit(solution)/shard_map/ppermute | solution.py:150
  47.1 4.0 %collective-permute-start.12 = (s16[208,512]{1,0:T(8,128)(2,1)S(1)}, s16[208,512]{1,0:T(8,128)(2,1)S(1)}, u32[]{:S(2)}, u32[]{:S(2)}) collective-permute-start(s16[208,512]{1,0:T(8,128)(2,1)S(1)} %get-tuple-element.24), channel_id=1, source_target_pairs={{0,7},{1,0},{2,1},{3,2},{4,3},{5,4},{6,5},{7,6},{8,15},{9,8},{10,9... | collective-permute-start | bytes 638984 | tf_op jit(solution)/shard_map/ppermute | solution.py:150
  51.1 5.0 %collective-permute-done.8.arrived = s16[208,512]{1,0:T(8,128)(2,1)S(1)} collective-permute-done((s16[208,512]{1,0:T(8,128)(2,1)S(1)}, s16[208,512]{1,0:T(8,128)(2,1)S(1)}, u32[]{:S(2)}, u32[]{:S(2)}) %collective-permute-start.8) | collective-permute-done | bytes 213024 | tf_op jit(solution)/shard_map/ppermute | solution.py:150
  56.8 3.5 %collective-permute-start.13 = (s16[208,512]{1,0:T(8,128)(2,1)S(1)}, s16[208,512]{1,0:T(8,128)(2,1)S(1)}, u32[]{:S(2)}, u32[]{:S(2)}) collective-permute-start(s16[208,512]{1,0:T(8,128)(2,1)S(1)} %hop.8), channel_id=1, source_target_pairs={{0,7},{1,0},{2,1},{3,2},{4,3},{5,4},{6,5},{7,6},{8,15},{9,8},{10,9... | collective-permute-start | bytes 638984 | tf_op jit(solution)/shard_map/ppermute | solution.py:150
  60.2 3.7 %collective-permute-done.9.arrived = s16[208,512]{1,0:T(8,128)(2,1)S(1)} collective-permute-done((s16[208,512]{1,0:T(8,128)(2,1)S(1)}, s16[208,512]{1,0:T(8,128)(2,1)S(1)}, u32[]{:S(2)}, u32[]{:S(2)}) %collective-permute-start.9) | collective-permute-done | bytes 213024 | tf_op jit(solution)/shard_map/ppermute | solution.py:150
  64.6 3.3 %collective-permute-start.14 = (s16[208,512]{1,0:T(8,128)(2,1)S(1)}, s16[208,512]{1,0:T(8,128)(2,1)S(1)}, u32[]{:S(2)}, u32[]{:S(2)}) collective-permute-start(s16[208,512]{1,0:T(8,128)(2,1)S(1)} %hop.9), channel_id=1, source_target_pairs={{0,7},{1,0},{2,1},{3,2},{4,3},{5,4},{6,5},{7,6},{8,15},{9,8},{10,9... | collective-permute-start | bytes 638984 | tf_op jit(solution)/shard_map/ppermute | solution.py:150
  67.9 3.5 %collective-permute-done.10.arrived = s16[208,512]{1,0:T(8,128)(2,1)S(1)} collective-permute-done((s16[208,512]{1,0:T(8,128)(2,1)S(1)}, s16[208,512]{1,0:T(8,128)(2,1)S(1)}, u32[]{:S(2)}, u32[]{:S(2)}) %collective-permute-start.10) | collective-permute-done | bytes 213024 | tf_op jit(solution)/shard_map/ppermute | solution.py:150
  71.7 7.0 %collective-permute-done.11.up = s16[208,512]{1,0:T(8,128)(2,1)S(1)} collective-permute-done((s16[208,512]{1,0:T(8,128)(2,1)S(1)}, s16[208,512]{1,0:T(8,128)(2,1)S(1)}, u32[]{:S(2)}, u32[]{:S(2)}) %collective-permute-start.11) | collective-permute-done | bytes 213024 | tf_op jit(solution)/shard_map/ppermute | solution.py:150
  79.0 3.5 %collective-permute-start.16 = (bf16[48,512]{1,0:T(8,128)(2,1)S(1)}, bf16[48,512]{1,0:T(8,128)(2,1)S(1)}, u32[]{:S(2)}, u32[]{:S(2)}) collective-permute-start(bf16[48,512]{1,0:T(8,128)(2,1)S(1)} %get-tuple-element.27), channel_id=1, source_target_pairs={{0,16},{8,24},{16,0},{24,8},{1,17},{9,25},{17,1},{25,9},{2,18},{10... | collective-permute-start | bytes 147464 | tf_op jit(solution)/shard_map/ppermute | solution.py:146
  83.7 1.4 %collective-permute-done.16.refs_2_ = bf16[48,512]{1,0:T(8,128)(2,1)S(1)} collective-permute-done((bf16[48,512]{1,0:T(8,128)(2,1)S(1)}, bf16[48,512]{1,0:T(8,128)(2,1)S(1)}, u32[]{:S(2)}, u32[]{:S(2)}) %collective-permute-start.16) | collective-permute-done | bytes 49184 | tf_op jit(solution)/shard_map/ppermute | solution.py:146
  85.1 2.7 %collective-permute-done.17.refs_3_ = bf16[48,512]{1,0:T(8,128)(2,1)S(1)} collective-permute-done((bf16[48,512]{1,0:T(8,128)(2,1)S(1)}, bf16[48,512]{1,0:T(8,128)(2,1)S(1)}, u32[]{:S(2)}, u32[]{:S(2)}) %collective-permute-start.17) | collective-permute-done | bytes 49184 | tf_op jit(solution)/shard_map/ppermute | solution.py:146
  (59 shorter events, 11.9 us)
Async XLA Ops:
  0.0 7.8 %copy-start.5 = (s32[1,1,8,1,4]{2,4,3,1,0:T(4,128)S(1)}, s32[1,1,8,1,4]{2,4,3,1,0:T(4,128)}, u32[]{:S(2)}) copy-start(s32[1,1,8,1,4]{2,4,3,1,0:T(4,128)} %param.14) | copy-start | bytes 388
  0.0 7.8 %copy-start.6 = (s32[1,1,8,1]{2,3,1,0:T(1,128)S(1)}, s32[1,1,8,1]{2,3,1,0:T(1,128)}, u32[]{:S(2)}) copy-start(s32[1,1,8,1]{2,3,1,0:T(1,128)} %param.15) | copy-start | bytes 100
  0.0 8.2 %copy-start.4 = (bf16[1,1,8,1,64,256]{5,4,3,2,1,0:T(8,128)(2,1)S(1)}, bf16[1,1,8,1,64,256]{5,4,3,2,1,0:T(8,128)(2,1)}, u32[]{:S(2)}) copy-start(bf16[1,1,8,1,64,256]{5,4,3,2,1,0:T(8,128)(2,1)} %param.13) | copy-start | bytes 786436
  4.1 20.2 %collective-permute-start.3 = (bf16[3088,128]{1,0:T(8,128)(2,1)S(1)}, bf16[3088,128]{1,0:T(8,128)(2,1)S(1)}, u32[]{:S(2)}, u32[]{:S(2)}) collective-permute-start(bf16[3088,128]{1,0:T(8,128)(2,1)S(1)} %fusion.1.refs_0_), channel_id=1, source_target_pairs={{0,8},{8,0},{16,24},{24,16},{1,9},{9,1},{17,25},{25,17},{2,10},{10... | collective-permute-start | bytes 2371592 | tf_op jit(solution)/shard_map/ppermute | solution.py:146
  5.7 20.3 %collective-permute-start.4 = (bf16[3088,128]{1,0:T(8,128)(2,1)S(1)}, bf16[3088,128]{1,0:T(8,128)(2,1)S(1)}, u32[]{:S(2)}, u32[]{:S(2)}) collective-permute-start(bf16[3088,128]{1,0:T(8,128)(2,1)S(1)} %fusion.1.refs_0_), channel_id=1, source_target_pairs={{0,24},{8,16},{16,8},{24,0},{1,25},{9,17},{17,9},{25,1},{2,26},{10... | collective-permute-start | bytes 2371592 | tf_op jit(solution)/shard_map/ppermute | solution.py:146
  8.3 9.5 %collective-permute-start = (bf16[528,256]{1,0:T(8,128)(2,1)S(1)}, bf16[528,256]{1,0:T(8,128)(2,1)S(1)}, u32[]{:S(2)}, u32[]{:S(2)}) collective-permute-start(bf16[528,256]{1,0:T(8,128)(2,1)S(1)} %get-tuple-element.32), channel_id=1, source_target_pairs={{0,64},{32,96},{64,0},{96,32},{128,192},{160,224},{192,128},{224,1... | collective-permute-start | bytes 811016 | tf_op jit(solution)/shard_map/ppermute | solution.py:146
  8.8 14.1 %collective-permute-start.1 = (bf16[528,256]{1,0:T(8,128)(2,1)S(1)}, bf16[528,256]{1,0:T(8,128)(2,1)S(1)}, u32[]{:S(2)}, u32[]{:S(2)}) collective-permute-start(bf16[528,256]{1,0:T(8,128)(2,1)S(1)} %get-tuple-element.32), channel_id=1, source_target_pairs={{0,128},{32,160},{64,192},{96,224},{128,0},{160,32},{192,64},{224,... | collective-permute-start | bytes 811016 | tf_op jit(solution)/shard_map/ppermute | solution.py:146
  11.4 12.9 %collective-permute-start.2 = (bf16[528,256]{1,0:T(8,128)(2,1)S(1)}, bf16[528,256]{1,0:T(8,128)(2,1)S(1)}, u32[]{:S(2)}, u32[]{:S(2)}) collective-permute-start(bf16[528,256]{1,0:T(8,128)(2,1)S(1)} %get-tuple-element.32), channel_id=1, source_target_pairs={{0,192},{32,224},{64,128},{96,160},{128,64},{160,96},{192,0},{224,... | collective-permute-start | bytes 811016 | tf_op jit(solution)/shard_map/ppermute | solution.py:146
  24.3 1.7 %copy-start = (bf16[3088,128]{1,0:T(8,128)(2,1)}, bf16[3088,128]{1,0:T(8,128)(2,1)S(1)}, u32[]{:S(2)}) copy-start(bf16[3088,128]{1,0:T(8,128)(2,1)S(1)} %collective-permute-done.3.refs_1_) | copy-start | bytes 2371588
  27.1 4.2 %collective-permute-start.5 = (bf16[4,528,256]{2,1,0:T(8,128)(2,1)S(1)}, bf16[4,528,256]{2,1,0:T(8,128)(2,1)S(1)}, u32[]{:S(2)}, u32[]{:S(2)}) collective-permute-start(bf16[4,528,256]{2,1,0:T(8,128)(2,1)S(1)} %pad_maximum_fusion.p_ref), channel_id=1, source_target_pairs={{0,32},{32,0},{64,96},{96,64},{128,160},{160,128},{192,224},{224,1... | collective-permute-start | bytes 3244040 | tf_op jit(solution)/shard_map/ppermute | solution.py:146
  27.2 1.7 %copy-start.3 = (bf16[3088,128]{1,0:T(8,128)(2,1)S(1)}, bf16[3088,128]{1,0:T(8,128)(2,1)}, u32[]{:S(2)}) copy-start(bf16[3088,128]{1,0:T(8,128)(2,1)} %copy-done.2) | copy-start | bytes 2371588
  27.2 1.8 %copy-start.1 = (bf16[3088,128]{1,0:T(8,128)(2,1)S(1)}, bf16[3088,128]{1,0:T(8,128)(2,1)}, u32[]{:S(2)}) copy-start(bf16[3088,128]{1,0:T(8,128)(2,1)} %copy-done) | copy-start | bytes 2371588
  28.9 11.6 %collective-permute-start.6 = (bf16[1536,128]{1,0:T(8,128)(2,1)S(1)}, bf16[1536,128]{1,0:T(8,128)(2,1)S(1)}, u32[]{:S(2)}, u32[]{:S(2)}) collective-permute-start(bf16[1536,128]{1,0:T(8,128)(2,1)S(1)} %slice.6), channel_id=1, source_target_pairs={{0,8},{8,0},{16,24},{24,16},{1,9},{9,1},{17,25},{25,17},{2,10},{10... | collective-permute-start | bytes 1179656 | tf_op jit(solution)/shard_map/ppermute | solution.py:146
  29.1 12.9 %collective-permute-start.7 = (bf16[1552,128]{1,0:T(8,128)(2,1)S(1)}, bf16[1552,128]{1,0:T(8,128)(2,1)S(1)}, u32[]{:S(2)}, u32[]{:S(2)}) collective-permute-start(bf16[1552,128]{1,0:T(8,128)(2,1)S(1)} %slice.7), channel_id=1, source_target_pairs={{0,24},{8,16},{16,8},{24,0},{1,25},{9,17},{17,9},{25,1},{2,26},{10... | collective-permute-start | bytes 1191944 | tf_op jit(solution)/shard_map/ppermute | solution.py:146
  45.1 11.0 %collective-permute-start.8 = (s16[208,512]{1,0:T(8,128)(2,1)S(1)}, s16[208,512]{1,0:T(8,128)(2,1)S(1)}, u32[]{:S(2)}, u32[]{:S(2)}) collective-permute-start(s16[208,512]{1,0:T(8,128)(2,1)S(1)} %get-tuple-element.22), channel_id=1, source_target_pairs={{0,1},{1,2},{2,3},{3,4},{4,5},{5,6},{6,7},{7,0},{8,9},{9,10},{10,1... | collective-permute-start | bytes 638984 | tf_op jit(solution)/shard_map/ppermute | solution.py:150
  47.1 9.4 %collective-permute-start.12 = (s16[208,512]{1,0:T(8,128)(2,1)S(1)}, s16[208,512]{1,0:T(8,128)(2,1)S(1)}, u32[]{:S(2)}, u32[]{:S(2)}) collective-permute-start(s16[208,512]{1,0:T(8,128)(2,1)S(1)} %get-tuple-element.24), channel_id=1, source_target_pairs={{0,7},{1,0},{2,1},{3,2},{4,3},{5,4},{6,5},{7,6},{8,15},{9,8},{10,9... | collective-permute-start | bytes 638984 | tf_op jit(solution)/shard_map/ppermute | solution.py:150
  56.4 7.6 %collective-permute-start.9 = (s16[208,512]{1,0:T(8,128)(2,1)S(1)}, s16[208,512]{1,0:T(8,128)(2,1)S(1)}, u32[]{:S(2)}, u32[]{:S(2)}) collective-permute-start(s16[208,512]{1,0:T(8,128)(2,1)S(1)} %hop.5), channel_id=1, source_target_pairs={{0,1},{1,2},{2,3},{3,4},{4,5},{5,6},{6,7},{7,0},{8,9},{9,10},{10,1... | collective-permute-start | bytes 638984 | tf_op jit(solution)/shard_map/ppermute | solution.py:150
  56.8 7.5 %collective-permute-start.13 = (s16[208,512]{1,0:T(8,128)(2,1)S(1)}, s16[208,512]{1,0:T(8,128)(2,1)S(1)}, u32[]{:S(2)}, u32[]{:S(2)}) collective-permute-start(s16[208,512]{1,0:T(8,128)(2,1)S(1)} %hop.8), channel_id=1, source_target_pairs={{0,7},{1,0},{2,1},{3,2},{4,3},{5,4},{6,5},{7,6},{8,15},{9,8},{10,9... | collective-permute-start | bytes 638984 | tf_op jit(solution)/shard_map/ppermute | solution.py:150
  64.2 7.1 %collective-permute-start.10 = (s16[208,512]{1,0:T(8,128)(2,1)S(1)}, s16[208,512]{1,0:T(8,128)(2,1)S(1)}, u32[]{:S(2)}, u32[]{:S(2)}) collective-permute-start(s16[208,512]{1,0:T(8,128)(2,1)S(1)} %hop.6), channel_id=1, source_target_pairs={{0,1},{1,2},{2,3},{3,4},{4,5},{5,6},{6,7},{7,0},{8,9},{9,10},{10,1... | collective-permute-start | bytes 638984 | tf_op jit(solution)/shard_map/ppermute | solution.py:150
  64.6 7.1 %collective-permute-start.14 = (s16[208,512]{1,0:T(8,128)(2,1)S(1)}, s16[208,512]{1,0:T(8,128)(2,1)S(1)}, u32[]{:S(2)}, u32[]{:S(2)}) collective-permute-start(s16[208,512]{1,0:T(8,128)(2,1)S(1)} %hop.9), channel_id=1, source_target_pairs={{0,7},{1,0},{2,1},{3,2},{4,3},{5,4},{6,5},{7,6},{8,15},{9,8},{10,9... | collective-permute-start | bytes 638984 | tf_op jit(solution)/shard_map/ppermute | solution.py:150
  71.6 7.1 %collective-permute-start.11 = (s16[208,512]{1,0:T(8,128)(2,1)S(1)}, s16[208,512]{1,0:T(8,128)(2,1)S(1)}, u32[]{:S(2)}, u32[]{:S(2)}) collective-permute-start(s16[208,512]{1,0:T(8,128)(2,1)S(1)} %hop.7), channel_id=1, source_target_pairs={{0,1},{1,2},{2,3},{3,4},{4,5},{5,6},{6,7},{7,0},{8,9},{9,10},{10,1... | collective-permute-start | bytes 638984 | tf_op jit(solution)/shard_map/ppermute | solution.py:150
  78.9 4.8 %collective-permute-start.15 = (bf16[48,512]{1,0:T(8,128)(2,1)S(1)}, bf16[48,512]{1,0:T(8,128)(2,1)S(1)}, u32[]{:S(2)}, u32[]{:S(2)}) collective-permute-start(bf16[48,512]{1,0:T(8,128)(2,1)S(1)} %get-tuple-element.26), channel_id=1, source_target_pairs={{0,8},{8,0},{16,24},{24,16},{1,9},{9,1},{17,25},{25,17},{2,10},{10... | collective-permute-start | bytes 147464 | tf_op jit(solution)/shard_map/ppermute | solution.py:146
  79.0 6.1 %collective-permute-start.16 = (bf16[48,512]{1,0:T(8,128)(2,1)S(1)}, bf16[48,512]{1,0:T(8,128)(2,1)S(1)}, u32[]{:S(2)}, u32[]{:S(2)}) collective-permute-start(bf16[48,512]{1,0:T(8,128)(2,1)S(1)} %get-tuple-element.27), channel_id=1, source_target_pairs={{0,16},{8,24},{16,0},{24,8},{1,17},{9,25},{17,1},{25,9},{2,18},{10... | collective-permute-start | bytes 147464 | tf_op jit(solution)/shard_map/ppermute | solution.py:146
  82.5 5.3 %collective-permute-start.17 = (bf16[48,512]{1,0:T(8,128)(2,1)S(1)}, bf16[48,512]{1,0:T(8,128)(2,1)S(1)}, u32[]{:S(2)}, u32[]{:S(2)}) collective-permute-start(bf16[48,512]{1,0:T(8,128)(2,1)S(1)} %get-tuple-element.28), channel_id=1, source_target_pairs={{0,24},{8,16},{16,8},{24,0},{1,25},{9,17},{17,9},{25,1},{2,26},{10... | collective-permute-start | bytes 147464 | tf_op jit(solution)/shard_map/ppermute | solution.py:146
  (1 other events, 0.9 us)

commit v4 on v3

--- a/solution.py
+++ b/solution.py
@@ -15,34 +15,35 @@
 SMEM_SPEC = pl.BlockSpec(memory_space=pltpu.SMEM)
 
 
-def expand_kernel(core, row_ref, p_ref, *refs):
-    out_ref = refs[-1]
+def expand_kernel(row_ref, *refs):
+    p_refs, out_ref = refs[:2], refs[2]
     panels = out_ref.shape[0] // PANEL_ROWS
-    row = row_ref[0]
-
-    @pl.loop(0, p_ref.shape[0])
-    def _(n):
-        panel = row ^ (2 * n + core)
-        for w in range(PANEL_ROWS):
-            blocks = p_ref[n, w * 64:(w + 1) * 64, :]
-            sources, wanted = [], []
-            for half in range(2):
-                straight = blocks[:, half * 128:(half + 1) * 128]
-                swapped = jnp.concatenate([straight[:, 64:], straight[:, :64]], axis=1)
-                for side, source in enumerate((straight, swapped)):
-                    sources.append(source.reshape(4, 16, 128))
-                    r = PANEL_ROWS * 64 + 2 * w + half
-                    want = p_ref[n, r:r + 1, side * 128:(side + 1) * 128]
-                    wanted.append(jnp.broadcast_to(want.astype(F32), (16, 128)))
-            for j in range(4):
-                total = None
-                for source, want in zip(sources, wanted):
-                    term = source * jnp.where(want == 2.0 * j, 1.0, 0.0).astype(BF)[None]
-                    total = term if total is None else total + term
-                out_ref[panel * PANEL_ROWS + w, j] = total.reshape(64, 128)
-
-    if core:
-        out_ref[panels * PANEL_ROWS] = jnp.zeros(out_ref.shape[1:], BF)
+    for core, p_ref in enumerate(p_refs):
+        @pl.loop(0, p_ref.shape[0])
+        def _(n):
+            expand_panel(p_ref, n, row_ref[0] ^ (2 * n + core), out_ref)
+
+    out_ref[panels * PANEL_ROWS] = jnp.zeros(out_ref.shape[1:], BF)
+
+
+def expand_panel(p_ref, n, panel, out_ref):
+    for w in range(PANEL_ROWS):
+        blocks = p_ref[n, w * 64:(w + 1) * 64, :]
+        sources, wanted = [], []
+        for half in range(2):
+            straight = blocks[:, half * 128:(half + 1) * 128]
+            swapped = jnp.concatenate([straight[:, 64:], straight[:, :64]], axis=1)
+            for side, source in enumerate((straight, swapped)):
+                sources.append(source.reshape(4, 16, 128))
+                r = PANEL_ROWS * 64 + 2 * w + half
+                want = p_ref[n, r:r + 1, side * 128:(side + 1) * 128]
+                wanted.append(jnp.broadcast_to(want.astype(F32), (16, 128)))
+        for j in range(4):
+            total = None
+            for source, want in zip(sources, wanted):
+                term = source * jnp.where(want == 2.0 * j, 1.0, 0.0).astype(BF)[None]
+                total = term if total is None else total + term
+            out_ref[panel * PANEL_ROWS + w, j] = total.reshape(64, 128)
 
 
 def multiply(sums, add, k_ref, dense_ref, lefts):
@@ -57,7 +58,7 @@
                         first = ((i - base) * 2 + s) * 64
                         left.append(a_ref[pl.ds(pl.multiple_of(first, 64), 64), :])
                         for slot in range(2):
-                            k = k_ref[n, (i * 2 + s) * 2 + slot]
+                            k = k_ref[4 * n + 2 * s + slot, i]
                             right.append(jnp.concatenate([dense_ref[k, j] for j in range(4)], axis=1))
                 total = jnp.dot(
                     jnp.concatenate(left, axis=1), jnp.concatenate(right, axis=0), preferred_element_type=F32
@@ -69,9 +70,9 @@
                     sums[where] = sums[where] + term if add else term
 
 
-def load_k(k_rows, k_vector, k_ref, sem):
-    for n, k in enumerate(k_rows):
-        k_vector[n:n + 1] = k.astype(F32).astype(jnp.int32)
+def load_k(k_tiles, k_vector, k_ref, sem):
+    for n, k in enumerate(k_tiles):
+        k_vector[4 * n:4 * n + 4] = k.astype(F32).astype(jnp.int32)[0:4]
     copy = pltpu.make_async_copy(k_vector, k_ref, sem)
     copy.start()
     copy.wait()
@@ -80,7 +81,7 @@
 def near_kernel(*refs):
     a_refs, dense_ref, sums, scratch = refs[:3], refs[3], refs[4], refs[5:]
     count = a_refs[0].shape[0] - 16
-    load_k([a[count:count + 1] for a in a_refs], *scratch)
+    load_k([a[count:count + 16] for a in a_refs], *scratch)
     multiply(sums, False, scratch[1], dense_ref, lambda g: [(a, 0) for a in a_refs])
 
 
@@ -107,7 +108,7 @@
 def far_kernel(layer_ref, sums_in, first_ref, second_ref, dense_ref, sums, up, down, *scratch):
     count = second_ref.shape[0] - 16
     k_scratch, scales = scratch[:3], scratch[3]
-    load_k([second_ref[count:count + 1]], *k_scratch)
+    load_k([second_ref[count:count + 16]], *k_scratch)
     half = sums.shape[1] // 2
     multiply(
         sums, True, k_scratch[1], dense_ref,
@@ -158,19 +159,20 @@
     here = lax.axis_index("col")
     layer = lax.axis_index("layer")
     row = lax.axis_index("row")
-    layer_map = lax.dynamic_index_in_dim(panel_map, layer, 0, keepdims=False)
-    panels = lax.dynamic_slice_in_dim(layer_map, here * sections, sections, 0)
     panel_rows = p_vals.shape[2]
     fine = panel_map.shape[1] * panel_rows
 
+    a_flat = a_vals[:, 0].reshape(rows * sections * side, 2 * side)
+    p_flat = p_vals.reshape(panel_rows * side, p_cols.shape[4] * side)
+    panels = lax.dynamic_slice(panel_map, (layer, here * sections), (1, sections)).reshape(sections, 1, 1)
     slot_a = a_cols.shape[3]
-    k_index = jnp.where(
-        jnp.arange(slot_a) < a_count[:, 0, :, None],
-        panels[None, :, None] * panel_rows + a_cols[:, 0],
-        fine,
-    ).reshape(1, -1)
-    k_tile = jnp.pad(k_index.astype(BF), ((0, 15), (0, 2 * side - k_index.size)))
-    own = jnp.concatenate([a_vals[:, 0].reshape(rows * sections * side, 2 * side), k_tile], axis=0)
+    valid = jnp.arange(slot_a)[None, :, None] < a_count.transpose(1, 2, 0)[0][:, None, :]
+    k_index = jnp.where(valid, panels * panel_rows + a_cols.transpose(1, 2, 3, 0)[0], fine)
+    k_tile = jnp.pad(
+        k_index.astype(BF).reshape(sections * slot_a, rows), ((0, 16 - sections * slot_a), (0, 2 * side - rows))
+    )
+    own = jnp.concatenate([a_flat, k_tile], axis=0)
+
     from_left, from_right = swap(own, "col", cols, 1), swap(own, "col", cols, 3)
 
     slot_p = p_cols.shape[4]
@@ -178,36 +180,29 @@
     odd = index.reshape(panel_rows, 2, 2)
     odd = jnp.concatenate([odd - jnp.array([0, 1]), odd[:, :, ::-1] - jnp.array([0, 1])], axis=2)
     wanted = jnp.broadcast_to(odd[:, :, :, None].astype(BF), (panel_rows, 2, 4, side))
-    mine = jnp.concatenate(
-        [p_vals.reshape(panel_rows * side, slot_p * side), wanted.reshape(2 * panel_rows, 4 * side)], axis=0
-    )
+    mine = jnp.concatenate([p_flat, wanted.reshape(2 * panel_rows, 4 * side)], axis=0)
     p_line = [swap(mine, "row", grid_rows, mask) for mask in (2, 4, 6)]
-    p_line, from_left, from_right = lax.optimization_barrier((p_line, from_left, from_right))
+    cut = a_flat.shape[0] // 2
+    halves = [from_right[:cut], from_left[cut:]]
+    p_line, halves, from_left, from_right = lax.optimization_barrier((p_line, halves, from_left, from_right))
+    far_first, far_second = swap(halves[0], "col", cols, 1), swap(halves[1], "col", cols, 3)
     p_line = jnp.stack([mine] + p_line)
     p_pair = swap(p_line, "row", grid_rows, 1)
 
-    cut = rows * sections * side // 2
-    far_first = swap(from_right[:cut], "col", cols, 1)
-    far_second = swap(from_left[cut:], "col", cols, 3)
-
-    dense = []
-    for core, part in enumerate((p_line, p_pair)):
-        dense = [pl.pallas_call(
-            functools.partial(expand_kernel, core),
-            out_shape=jax.ShapeDtypeStruct((fine + 1, 4, side, 128), BF),
-            in_specs=[SMEM_SPEC] + [VMEM_SPEC] * (1 + core),
-            out_specs=VMEM_SPEC,
-            input_output_aliases={2: 0} if core else {},
-            name="expand",
-            compiler_params=pltpu.CompilerParams(vmem_limit_bytes=14 << 20),
-            cost_estimate=pl.CostEstimate(flops=0, bytes_accessed=10 << 20, transcendentals=0),
-        )(row.reshape(1), part, *dense)]
-    dense = dense[0]
+    dense = pl.pallas_call(
+        expand_kernel,
+        out_shape=jax.ShapeDtypeStruct((fine + 1, 4, side, 128), BF),
+        in_specs=[SMEM_SPEC] + [VMEM_SPEC] * 2,
+        out_specs=VMEM_SPEC,
+        name="expand",
+        compiler_params=pltpu.CompilerParams(vmem_limit_bytes=14 << 20),
+        cost_estimate=pl.CostEstimate(flops=0, bytes_accessed=10 << 20, transcendentals=0),
+    )(row.reshape(1), p_line, p_pair)
 
     width = CB * side
     sums_shape = jax.ShapeDtypeStruct((layers, rows // 6, 48, width), F32)
     coded = jax.ShapeDtypeStruct((208, width), jnp.int16)
-    k_scratch = [pltpu.VMEM((8, 128), jnp.int32), pltpu.SMEM((8, 128), jnp.int32), pltpu.SemaphoreType.DMA(())]
+    k_scratch = [pltpu.VMEM((16, 128), jnp.int32), pltpu.SMEM((16, 128), jnp.int32), pltpu.SemaphoreType.DMA(())]
     scales = pltpu.VMEM((16, width), F32)
     layer = layer.reshape(1)
     sums = pl.pallas_call(

time: 88.7 us -> 86.1 us (0.971)
  waiting for transfers between devices: 41.6 us -> 38.7 us
  local copies, waits for them, and re-layouts: 3.36 us -> 2.28 us
    ppermute x11, waiting for transfers between devices: 22.4 us -> 19.9 us  [swap(): return lax.ppermute(x, axis, [(n, n ^ mask) for n in range(size)])]
    unnamed x15 -> x14, local copies, waits for them, and re-layouts: 1.74 us -> 0.17 us
    pallas_call x2 -> x1, Pallas kernels: 3.3 us -> 3.3 us  [body(): pl.pallas_call(expand_kernel, out_shape=jax.ShapeDtypeStruct((fine + 1, 4...]
  transfers between devices with their start and end apart: 18 -> 18, of which waited for: 12 -> 11; matrix products, arithmetic and copies ran while one was open for 1% -> 2% of each run, Pallas kernels for 11% -> 11%
where the time goes in v4:
time: 86.1 us; the launch traced here: 85.9 us
  waiting for transfers between devices  38.7 us (45%)
  starting transfers between devices  28 us (33%)
  Pallas kernels  13.6 us (16%)
  other arithmetic  3.02 us (4%)
  local copies, waits for them, and re-layouts  2.28 us (3%)
    ppermute x11, waiting for transfers between devices, swap(): return lax.ppermute(x, axis, [(n, n ^ mask) for n in range(size)])  19.9 us
    ppermute x7, waiting for transfers between devices, shift(): return lax.ppermute(x, axis, [(n, (n + by) % size) for n in range(size)])  18.8 us
    ppermute x11, starting transfers between devices, swap(): return lax.ppermute(x, axis, [(n, n ^ mask) for n in range(size)])  15 us
    ppermute x7, starting transfers between devices, shift(): return lax.ppermute(x, axis, [(n, (n + by) % size) for n in range(size)])  13 us
    pallas_call x1, Pallas kernels, body(): pl.pallas_call(near_kernel, out_shape=sums_shape, in_specs=[VMEM_SPEC] *...  5 us
    pallas_call x1, Pallas kernels, body(): pl.pallas_call(expand_kernel, out_shape=jax.ShapeDtypeStruct((fine + 1, 4...  3.3 us
    pallas_call x1, Pallas kernels, body(): pl.pallas_call(far_kernel, out_shape=[sums_shape, coded, coded], in_specs...  3.2 us
  transfers between devices with their start and end apart: 18, of which 11 were waited for; matrix products, arithmetic and copies ran while one was open for 2% of the time, Pallas kernels for 11%

profile of v4, /device:TPU:8, one launch (start us, length us, event | category | flops | bytes accessed | tf_op | source)
XLA Modules:
  0.0 85.9 jit_solution(9462133106864299148)
XLA Ops:
  2.5 1.2 %fusion.1.refs_0_ = bf16[3088,128]{1,0:T(8,128)(2,1)S(1)} fusion(bf16[4,24]{1,0:T(4,128)(2,1)S(1)} %select_convert_fusion, bf16[3072,128]{1,0:T(8,128)(2,1)} %bitcast.21), kind=kLoop, calls=%fused_computation.3 | loop fusion | flops 2371584 | bytes 1577152 | tf_op jit(solution)/shard_map/concatenate | solution.py:174
  3.7 1.6 %collective-permute-start.4 = (bf16[3088,128]{1,0:T(8,128)(2,1)S(1)}, bf16[3088,128]{1,0:T(8,128)(2,1)S(1)}, u32[]{:S(2)}, u32[]{:S(2)}) collective-permute-start(bf16[3088,128]{1,0:T(8,128)(2,1)S(1)} %fusion.1.refs_0_), channel_id=1, source_target_pairs={{0,8},{8,0},{16,24},{24,16},{1,9},{9,1},{17,25},{25,17},{2,10},{10... | collective-permute-start | bytes 2371592 | tf_op jit(solution)/shard_map/ppermute | solution.py:147
  5.3 2.1 %collective-permute-start.3 = (bf16[3088,128]{1,0:T(8,128)(2,1)S(1)}, bf16[3088,128]{1,0:T(8,128)(2,1)S(1)}, u32[]{:S(2)}, u32[]{:S(2)}) collective-permute-start(bf16[3088,128]{1,0:T(8,128)(2,1)S(1)} %fusion.1.refs_0_), channel_id=1, source_target_pairs={{0,24},{8,16},{16,8},{24,0},{1,25},{9,17},{17,9},{25,1},{2,26},{10... | collective-permute-start | bytes 2371592 | tf_op jit(solution)/shard_map/ppermute | solution.py:147
  7.8 1.7 %collective-permute-start.2 = (bf16[528,256]{1,0:T(8,128)(2,1)S(1)}, bf16[528,256]{1,0:T(8,128)(2,1)S(1)}, u32[]{:S(2)}, u32[]{:S(2)}) collective-permute-start(bf16[528,256]{1,0:T(8,128)(2,1)S(1)} %get-tuple-element.36), channel_id=1, source_target_pairs={{0,192},{32,224},{64,128},{96,160},{128,64},{160,96},{192,0},{224,... | collective-permute-start | bytes 811016 | tf_op jit(solution)/shard_map/ppermute | solution.py:147
  10.4 1.6 %collective-permute-start = (bf16[528,256]{1,0:T(8,128)(2,1)S(1)}, bf16[528,256]{1,0:T(8,128)(2,1)S(1)}, u32[]{:S(2)}, u32[]{:S(2)}) collective-permute-start(bf16[528,256]{1,0:T(8,128)(2,1)S(1)} %get-tuple-element.36), channel_id=1, source_target_pairs={{0,64},{32,96},{64,0},{96,32},{128,192},{160,224},{192,128},{224,1... | collective-permute-start | bytes 811016 | tf_op jit(solution)/shard_map/ppermute | solution.py:147
  12.0 11.1 %collective-permute-done.4.refs_1_ = bf16[3088,128]{1,0:T(8,128)(2,1)S(1)} collective-permute-done((bf16[3088,128]{1,0:T(8,128)(2,1)S(1)}, bf16[3088,128]{1,0:T(8,128)(2,1)S(1)}, u32[]{:S(2)}, u32[]{:S(2)}) %collective-permute-start.4) | collective-permute-done | bytes 790560 | tf_op jit(solution)/shard_map/ppermute | solution.py:147
  23.2 2.4 %collective-permute-done.3.refs_2_ = bf16[3088,128]{1,0:T(8,128)(2,1)S(1)} collective-permute-done((bf16[3088,128]{1,0:T(8,128)(2,1)S(1)}, bf16[3088,128]{1,0:T(8,128)(2,1)S(1)}, u32[]{:S(2)}, u32[]{:S(2)}) %collective-permute-start.3) | collective-permute-done | bytes 790560 | tf_op jit(solution)/shard_map/ppermute | solution.py:147
  26.9 2.2 %collective-permute-start.7 = (bf16[1552,128]{1,0:T(8,128)(2,1)S(1)}, bf16[1552,128]{1,0:T(8,128)(2,1)S(1)}, u32[]{:S(2)}, u32[]{:S(2)}) collective-permute-start(bf16[1552,128]{1,0:T(8,128)(2,1)S(1)} %slice.9), channel_id=1, source_target_pairs={{0,24},{8,16},{16,8},{24,0},{1,25},{9,17},{17,9},{25,1},{2,26},{10... | collective-permute-start | bytes 1191944 | tf_op jit(solution)/shard_map/ppermute | solution.py:147
  29.5 3.3 %expand.1.refs_3_.dense_ref = bf16[65,4,64,128]{3,2,1,0:T(8,128)(2,1)S(1)} custom-call(s32[1]{0:T(128)} %bitcast.12.row_ref, bf16[4,528,256]{2,1,0:T(8,128)(2,1)S(1)} %pad_maximum_fusion.refs_0_, bf16[4,528,256]{2,1,0:T(8,128)(2,1)S(1)} %collective-permute-done.5.refs_1_), custom_call_target="tpu_custom_call" | custom-call | bytes 10485760 | tf_op jit(solution)/shard_map/expand/pallas_call | solution.py:192
  32.9 5.0 %near.1.sums_in = f32[8,4,48,512]{3,2,1,0:T(8,128)S(1)} custom-call(bf16[3088,128]{1,0:T(8,128)(2,1)S(1)} %fusion.1.refs_0_, bf16[3088,128]{1,0:T(8,128)(2,1)S(1)} %copy-done.1, bf16[3088,128]{1,0:T(8,128)(2,1)S(1)} %copy-done.3, bf16[65,4,64,128]{3,2,1,0:T(8,128)(2,1)S(1)} %expand.1.refs_3_.dense_ref), custom_call_target="tpu_custom_call" | custom-call | flops 4294967296 | bytes 11534336 | tf_op jit(solution)/shard_map/near/pallas_call | solution.py:208
  38.6 1.1 %collective-permute-done.7.second_ref = bf16[1552,128]{1,0:T(8,128)(2,1)S(1)} collective-permute-done((bf16[1552,128]{1,0:T(8,128)(2,1)S(1)}, bf16[1552,128]{1,0:T(8,128)(2,1)S(1)}, u32[]{:S(2)}, u32[]{:S(2)}) %collective-permute-start.7) | collective-permute-done | bytes 397344 | tf_op jit(solution)/shard_map/ppermute | solution.py:147
  39.7 3.2 %far.1 = (f32[8,4,48,512]{3,2,1,0:T(8,128)S(1)}, s16[208,512]{1,0:T(8,128)(2,1)S(1)}, s16[208,512]{1,0:T(8,128)(2,1)S(1)}) custom-call(s32[1]{0:T(128)} %bitcast.1.layer_ref, f32[8,4,48,512]{3,2,1,0:T(8,128)S(1)} %near.1.sums_in, bf16[1536,128]{1,0:T(8,128)(2,1)S(1)} %collective-permute-done.6.first_ref, ...), custom_call_target="tpu_custom_call", output_to_operand_aliasing={{0}: (1, {})} | custom-call | flops 1073741824 | bytes 9437184 | tf_op jit(solution)/shard_map/far/pallas_call | solution.py:218
  42.9 2.0 %collective-permute-start.8 = (s16[208,512]{1,0:T(8,128)(2,1)S(1)}, s16[208,512]{1,0:T(8,128)(2,1)S(1)}, u32[]{:S(2)}, u32[]{:S(2)}) collective-permute-start(s16[208,512]{1,0:T(8,128)(2,1)S(1)} %get-tuple-element.26), channel_id=1, source_target_pairs={{0,1},{1,2},{2,3},{3,4},{4,5},{5,6},{6,7},{7,0},{8,9},{9,10},{10,1... | collective-permute-start | bytes 638984 | tf_op jit(solution)/shard_map/ppermute | solution.py:151
  44.9 4.0 %collective-permute-start.12 = (s16[208,512]{1,0:T(8,128)(2,1)S(1)}, s16[208,512]{1,0:T(8,128)(2,1)S(1)}, u32[]{:S(2)}, u32[]{:S(2)}) collective-permute-start(s16[208,512]{1,0:T(8,128)(2,1)S(1)} %get-tuple-element.28), channel_id=1, source_target_pairs={{0,7},{1,0},{2,1},{3,2},{4,3},{5,4},{6,5},{7,6},{8,15},{9,8},{10,9... | collective-permute-start | bytes 638984 | tf_op jit(solution)/shard_map/ppermute | solution.py:151
  48.9 4.8 %collective-permute-done.8.arrived = s16[208,512]{1,0:T(8,128)(2,1)S(1)} collective-permute-done((s16[208,512]{1,0:T(8,128)(2,1)S(1)}, s16[208,512]{1,0:T(8,128)(2,1)S(1)}, u32[]{:S(2)}, u32[]{:S(2)}) %collective-permute-start.8) | collective-permute-done | bytes 213024 | tf_op jit(solution)/shard_map/ppermute | solution.py:151
  54.3 3.5 %collective-permute-start.13 = (s16[208,512]{1,0:T(8,128)(2,1)S(1)}, s16[208,512]{1,0:T(8,128)(2,1)S(1)}, u32[]{:S(2)}, u32[]{:S(2)}) collective-permute-start(s16[208,512]{1,0:T(8,128)(2,1)S(1)} %hop.8), channel_id=1, source_target_pairs={{0,7},{1,0},{2,1},{3,2},{4,3},{5,4},{6,5},{7,6},{8,15},{9,8},{10,9... | collective-permute-start | bytes 638984 | tf_op jit(solution)/shard_map/ppermute | solution.py:151
  57.8 3.5 %collective-permute-done.9.arrived = s16[208,512]{1,0:T(8,128)(2,1)S(1)} collective-permute-done((s16[208,512]{1,0:T(8,128)(2,1)S(1)}, s16[208,512]{1,0:T(8,128)(2,1)S(1)}, u32[]{:S(2)}, u32[]{:S(2)}) %collective-permute-start.9) | collective-permute-done | bytes 213024 | tf_op jit(solution)/shard_map/ppermute | solution.py:151
  62.0 3.3 %collective-permute-start.14 = (s16[208,512]{1,0:T(8,128)(2,1)S(1)}, s16[208,512]{1,0:T(8,128)(2,1)S(1)}, u32[]{:S(2)}, u32[]{:S(2)}) collective-permute-start(s16[208,512]{1,0:T(8,128)(2,1)S(1)} %hop.9), channel_id=1, source_target_pairs={{0,7},{1,0},{2,1},{3,2},{4,3},{5,4},{6,5},{7,6},{8,15},{9,8},{10,9... | collective-permute-start | bytes 638984 | tf_op jit(solution)/shard_map/ppermute | solution.py:151
  65.2 3.5 %collective-permute-done.10.arrived = s16[208,512]{1,0:T(8,128)(2,1)S(1)} collective-permute-done((s16[208,512]{1,0:T(8,128)(2,1)S(1)}, s16[208,512]{1,0:T(8,128)(2,1)S(1)}, u32[]{:S(2)}, u32[]{:S(2)}) %collective-permute-start.10) | collective-permute-done | bytes 213024 | tf_op jit(solution)/shard_map/ppermute | solution.py:151
  69.1 7.0 %collective-permute-done.11.up = s16[208,512]{1,0:T(8,128)(2,1)S(1)} collective-permute-done((s16[208,512]{1,0:T(8,128)(2,1)S(1)}, s16[208,512]{1,0:T(8,128)(2,1)S(1)}, u32[]{:S(2)}, u32[]{:S(2)}) %collective-permute-start.11) | collective-permute-done | bytes 213024 | tf_op jit(solution)/shard_map/ppermute | solution.py:151
  76.5 3.4 %collective-permute-start.16 = (bf16[48,512]{1,0:T(8,128)(2,1)S(1)}, bf16[48,512]{1,0:T(8,128)(2,1)S(1)}, u32[]{:S(2)}, u32[]{:S(2)}) collective-permute-start(bf16[48,512]{1,0:T(8,128)(2,1)S(1)} %get-tuple-element.31), channel_id=1, source_target_pairs={{0,16},{8,24},{16,0},{24,8},{1,17},{9,25},{17,1},{25,9},{2,18},{10... | collective-permute-start | bytes 147464 | tf_op jit(solution)/shard_map/ppermute | solution.py:147
  79.9 1.1 %collective-permute-start.17 = (bf16[48,512]{1,0:T(8,128)(2,1)S(1)}, bf16[48,512]{1,0:T(8,128)(2,1)S(1)}, u32[]{:S(2)}, u32[]{:S(2)}) collective-permute-start(bf16[48,512]{1,0:T(8,128)(2,1)S(1)} %get-tuple-element.32), channel_id=1, source_target_pairs={{0,24},{8,16},{16,8},{24,0},{1,25},{9,17},{17,9},{25,1},{2,26},{10... | collective-permute-start | bytes 147464 | tf_op jit(solution)/shard_map/ppermute | solution.py:147
  81.1 1.4 %collective-permute-done.16.refs_2_ = bf16[48,512]{1,0:T(8,128)(2,1)S(1)} collective-permute-done((bf16[48,512]{1,0:T(8,128)(2,1)S(1)}, bf16[48,512]{1,0:T(8,128)(2,1)S(1)}, u32[]{:S(2)}, u32[]{:S(2)}) %collective-permute-start.16) | collective-permute-done | bytes 49184 | tf_op jit(solution)/shard_map/ppermute | solution.py:147
  82.5 2.7 %collective-permute-done.17.refs_3_ = bf16[48,512]{1,0:T(8,128)(2,1)S(1)} collective-permute-done((bf16[48,512]{1,0:T(8,128)(2,1)S(1)}, bf16[48,512]{1,0:T(8,128)(2,1)S(1)}, u32[]{:S(2)}, u32[]{:S(2)}) %collective-permute-start.17) | collective-permute-done | bytes 49184 | tf_op jit(solution)/shard_map/ppermute | solution.py:147
  (56 shorter events, 9.1 us)
Async XLA Ops:
  0.0 7.4 %copy-start.6 = (s32[1,1,8,1]{2,3,1,0:T(1,128)S(1)}, s32[1,1,8,1]{2,3,1,0:T(1,128)}, u32[]{:S(2)}) copy-start(s32[1,1,8,1]{2,3,1,0:T(1,128)} %param.15) | copy-start | bytes 100
  0.0 7.4 %copy-start.5 = (s32[1,1,8,1,4]{2,4,3,1,0:T(4,128)S(1)}, s32[1,1,8,1,4]{2,4,3,1,0:T(4,128)}, u32[]{:S(2)}) copy-start(s32[1,1,8,1,4]{2,4,3,1,0:T(4,128)} %param.14) | copy-start | bytes 388
  0.0 7.8 %copy-start.4 = (bf16[1,1,8,1,64,256]{5,4,3,2,1,0:T(8,128)(2,1)S(1)}, bf16[1,1,8,1,64,256]{5,4,3,2,1,0:T(8,128)(2,1)}, u32[]{:S(2)}) copy-start(bf16[1,1,8,1,64,256]{5,4,3,2,1,0:T(8,128)(2,1)} %param.13) | copy-start | bytes 786436
  3.7 19.5 %collective-permute-start.4 = (bf16[3088,128]{1,0:T(8,128)(2,1)S(1)}, bf16[3088,128]{1,0:T(8,128)(2,1)S(1)}, u32[]{:S(2)}, u32[]{:S(2)}) collective-permute-start(bf16[3088,128]{1,0:T(8,128)(2,1)S(1)} %fusion.1.refs_0_), channel_id=1, source_target_pairs={{0,8},{8,0},{16,24},{24,16},{1,9},{9,1},{17,25},{25,17},{2,10},{10... | collective-permute-start | bytes 2371592 | tf_op jit(solution)/shard_map/ppermute | solution.py:147
  5.3 20.3 %collective-permute-start.3 = (bf16[3088,128]{1,0:T(8,128)(2,1)S(1)}, bf16[3088,128]{1,0:T(8,128)(2,1)S(1)}, u32[]{:S(2)}, u32[]{:S(2)}) collective-permute-start(bf16[3088,128]{1,0:T(8,128)(2,1)S(1)} %fusion.1.refs_0_), channel_id=1, source_target_pairs={{0,24},{8,16},{16,8},{24,0},{1,25},{9,17},{17,9},{25,1},{2,26},{10... | collective-permute-start | bytes 2371592 | tf_op jit(solution)/shard_map/ppermute | solution.py:147
  7.8 18.6 %collective-permute-start.2 = (bf16[528,256]{1,0:T(8,128)(2,1)S(1)}, bf16[528,256]{1,0:T(8,128)(2,1)S(1)}, u32[]{:S(2)}, u32[]{:S(2)}) collective-permute-start(bf16[528,256]{1,0:T(8,128)(2,1)S(1)} %get-tuple-element.36), channel_id=1, source_target_pairs={{0,192},{32,224},{64,128},{96,160},{128,64},{160,96},{192,0},{224,... | collective-permute-start | bytes 811016 | tf_op jit(solution)/shard_map/ppermute | solution.py:147
  9.5 16.9 %collective-permute-start.1 = (bf16[528,256]{1,0:T(8,128)(2,1)S(1)}, bf16[528,256]{1,0:T(8,128)(2,1)S(1)}, u32[]{:S(2)}, u32[]{:S(2)}) collective-permute-start(bf16[528,256]{1,0:T(8,128)(2,1)S(1)} %get-tuple-element.36), channel_id=1, source_target_pairs={{0,128},{32,160},{64,192},{96,224},{128,0},{160,32},{192,64},{224,... | collective-permute-start | bytes 811016 | tf_op jit(solution)/shard_map/ppermute | solution.py:147
  10.4 16.0 %collective-permute-start = (bf16[528,256]{1,0:T(8,128)(2,1)S(1)}, bf16[528,256]{1,0:T(8,128)(2,1)S(1)}, u32[]{:S(2)}, u32[]{:S(2)}) collective-permute-start(bf16[528,256]{1,0:T(8,128)(2,1)S(1)} %get-tuple-element.36), channel_id=1, source_target_pairs={{0,64},{32,96},{64,0},{96,32},{128,192},{160,224},{192,128},{224,1... | collective-permute-start | bytes 811016 | tf_op jit(solution)/shard_map/ppermute | solution.py:147
  23.2 3.3 %copy-start = (bf16[3088,128]{1,0:T(8,128)(2,1)}, bf16[3088,128]{1,0:T(8,128)(2,1)S(1)}, u32[]{:S(2)}) copy-start(bf16[3088,128]{1,0:T(8,128)(2,1)S(1)} %collective-permute-done.4.refs_1_) | copy-start | bytes 2371588
  26.7 2.8 %collective-permute-start.5 = (bf16[4,528,256]{2,1,0:T(8,128)(2,1)S(1)}, bf16[4,528,256]{2,1,0:T(8,128)(2,1)S(1)}, u32[]{:S(2)}, u32[]{:S(2)}) collective-permute-start(bf16[4,528,256]{2,1,0:T(8,128)(2,1)S(1)} %pad_maximum_fusion.refs_0_), channel_id=1, source_target_pairs={{0,32},{32,0},{64,96},{96,64},{128,160},{160,128},{192,224},{224,1... | collective-permute-start | bytes 3244040 | tf_op jit(solution)/shard_map/ppermute | solution.py:147
  26.8 11.7 %collective-permute-start.6 = (bf16[1536,128]{1,0:T(8,128)(2,1)}, bf16[1536,128]{1,0:T(8,128)(2,1)S(1)}, u32[]{:S(2)}, u32[]{:S(2)}) collective-permute-start(bf16[1536,128]{1,0:T(8,128)(2,1)} %slice.8), channel_id=1, source_target_pairs={{0,8},{8,0},{16,24},{24,16},{1,9},{9,1},{17,25},{25,17},{2,10},{10... | collective-permute-start | bytes 1179656 | tf_op jit(solution)/shard_map/ppermute | solution.py:147
  26.9 12.7 %collective-permute-start.7 = (bf16[1552,128]{1,0:T(8,128)(2,1)S(1)}, bf16[1552,128]{1,0:T(8,128)(2,1)S(1)}, u32[]{:S(2)}, u32[]{:S(2)}) collective-permute-start(bf16[1552,128]{1,0:T(8,128)(2,1)S(1)} %slice.9), channel_id=1, source_target_pairs={{0,24},{8,16},{16,8},{24,0},{1,25},{9,17},{17,9},{25,1},{2,26},{10... | collective-permute-start | bytes 1191944 | tf_op jit(solution)/shard_map/ppermute | solution.py:147
  29.5 3.3 %copy-start.1 = (bf16[3088,128]{1,0:T(8,128)(2,1)S(1)}, bf16[3088,128]{1,0:T(8,128)(2,1)}, u32[]{:S(2)}) copy-start(bf16[3088,128]{1,0:T(8,128)(2,1)} %copy-done) | copy-start | bytes 2371588
  29.5 3.3 %copy-start.3 = (bf16[3088,128]{1,0:T(8,128)(2,1)S(1)}, bf16[3088,128]{1,0:T(8,128)(2,1)}, u32[]{:S(2)}) copy-start(bf16[3088,128]{1,0:T(8,128)(2,1)} %copy-done.2) | copy-start | bytes 2371588
  42.9 10.8 %collective-permute-start.8 = (s16[208,512]{1,0:T(8,128)(2,1)S(1)}, s16[208,512]{1,0:T(8,128)(2,1)S(1)}, u32[]{:S(2)}, u32[]{:S(2)}) collective-permute-start(s16[208,512]{1,0:T(8,128)(2,1)S(1)} %get-tuple-element.26), channel_id=1, source_target_pairs={{0,1},{1,2},{2,3},{3,4},{4,5},{5,6},{6,7},{7,0},{8,9},{9,10},{10,1... | collective-permute-start | bytes 638984 | tf_op jit(solution)/shard_map/ppermute | solution.py:151
  44.9 9.2 %collective-permute-start.12 = (s16[208,512]{1,0:T(8,128)(2,1)S(1)}, s16[208,512]{1,0:T(8,128)(2,1)S(1)}, u32[]{:S(2)}, u32[]{:S(2)}) collective-permute-start(s16[208,512]{1,0:T(8,128)(2,1)S(1)} %get-tuple-element.28), channel_id=1, source_target_pairs={{0,7},{1,0},{2,1},{3,2},{4,3},{5,4},{6,5},{7,6},{8,15},{9,8},{10,9... | collective-permute-start | bytes 638984 | tf_op jit(solution)/shard_map/ppermute | solution.py:151
  54.0 7.3 %collective-permute-start.9 = (s16[208,512]{1,0:T(8,128)(2,1)S(1)}, s16[208,512]{1,0:T(8,128)(2,1)S(1)}, u32[]{:S(2)}, u32[]{:S(2)}) collective-permute-start(s16[208,512]{1,0:T(8,128)(2,1)S(1)} %hop.5), channel_id=1, source_target_pairs={{0,1},{1,2},{2,3},{3,4},{4,5},{5,6},{6,7},{7,0},{8,9},{9,10},{10,1... | collective-permute-start | bytes 638984 | tf_op jit(solution)/shard_map/ppermute | solution.py:151
  54.3 7.3 %collective-permute-start.13 = (s16[208,512]{1,0:T(8,128)(2,1)S(1)}, s16[208,512]{1,0:T(8,128)(2,1)S(1)}, u32[]{:S(2)}, u32[]{:S(2)}) collective-permute-start(s16[208,512]{1,0:T(8,128)(2,1)S(1)} %hop.8), channel_id=1, source_target_pairs={{0,7},{1,0},{2,1},{3,2},{4,3},{5,4},{6,5},{7,6},{8,15},{9,8},{10,9... | collective-permute-start | bytes 638984 | tf_op jit(solution)/shard_map/ppermute | solution.py:151
  61.6 7.1 %collective-permute-start.10 = (s16[208,512]{1,0:T(8,128)(2,1)S(1)}, s16[208,512]{1,0:T(8,128)(2,1)S(1)}, u32[]{:S(2)}, u32[]{:S(2)}) collective-permute-start(s16[208,512]{1,0:T(8,128)(2,1)S(1)} %hop.6), channel_id=1, source_target_pairs={{0,1},{1,2},{2,3},{3,4},{4,5},{5,6},{6,7},{7,0},{8,9},{9,10},{10,1... | collective-permute-start | bytes 638984 | tf_op jit(solution)/shard_map/ppermute | solution.py:151
  62.0 7.1 %collective-permute-start.14 = (s16[208,512]{1,0:T(8,128)(2,1)S(1)}, s16[208,512]{1,0:T(8,128)(2,1)S(1)}, u32[]{:S(2)}, u32[]{:S(2)}) collective-permute-start(s16[208,512]{1,0:T(8,128)(2,1)S(1)} %hop.9), channel_id=1, source_target_pairs={{0,7},{1,0},{2,1},{3,2},{4,3},{5,4},{6,5},{7,6},{8,15},{9,8},{10,9... | collective-permute-start | bytes 638984 | tf_op jit(solution)/shard_map/ppermute | solution.py:151
  69.0 7.1 %collective-permute-start.11 = (s16[208,512]{1,0:T(8,128)(2,1)S(1)}, s16[208,512]{1,0:T(8,128)(2,1)S(1)}, u32[]{:S(2)}, u32[]{:S(2)}) collective-permute-start(s16[208,512]{1,0:T(8,128)(2,1)S(1)} %hop.7), channel_id=1, source_target_pairs={{0,1},{1,2},{2,3},{3,4},{4,5},{5,6},{6,7},{7,0},{8,9},{9,10},{10,1... | collective-permute-start | bytes 638984 | tf_op jit(solution)/shard_map/ppermute | solution.py:151
  76.3 4.8 %collective-permute-start.15 = (bf16[48,512]{1,0:T(8,128)(2,1)S(1)}, bf16[48,512]{1,0:T(8,128)(2,1)S(1)}, u32[]{:S(2)}, u32[]{:S(2)}) collective-permute-start(bf16[48,512]{1,0:T(8,128)(2,1)S(1)} %get-tuple-element.30), channel_id=1, source_target_pairs={{0,8},{8,0},{16,24},{24,16},{1,9},{9,1},{17,25},{25,17},{2,10},{10... | collective-permute-start | bytes 147464 | tf_op jit(solution)/shard_map/ppermute | solution.py:147
  76.5 6.0 %collective-permute-start.16 = (bf16[48,512]{1,0:T(8,128)(2,1)S(1)}, bf16[48,512]{1,0:T(8,128)(2,1)S(1)}, u32[]{:S(2)}, u32[]{:S(2)}) collective-permute-start(bf16[48,512]{1,0:T(8,128)(2,1)S(1)} %get-tuple-element.31), channel_id=1, source_target_pairs={{0,16},{8,24},{16,0},{24,8},{1,17},{9,25},{17,1},{25,9},{2,18},{10... | collective-permute-start | bytes 147464 | tf_op jit(solution)/shard_map/ppermute | solution.py:147
  79.9 5.3 %collective-permute-start.17 = (bf16[48,512]{1,0:T(8,128)(2,1)S(1)}, bf16[48,512]{1,0:T(8,128)(2,1)S(1)}, u32[]{:S(2)}, u32[]{:S(2)}) collective-permute-start(bf16[48,512]{1,0:T(8,128)(2,1)S(1)} %get-tuple-element.32), channel_id=1, source_target_pairs={{0,24},{8,16},{16,8},{24,0},{1,25},{9,17},{17,9},{25,1},{2,26},{10... | collective-permute-start | bytes 147464 | tf_op jit(solution)/shard_map/ppermute | solution.py:147
  (1 other events, 1.0 us)

commit v5 on v4

--- a/solution.py
+++ b/solution.py
@@ -166,11 +166,12 @@
     p_flat = p_vals.reshape(panel_rows * side, p_cols.shape[4] * side)
     panels = lax.dynamic_slice(panel_map, (layer, here * sections), (1, sections)).reshape(sections, 1, 1)
     slot_a = a_cols.shape[3]
-    valid = jnp.arange(slot_a)[None, :, None] < a_count.transpose(1, 2, 0)[0][:, None, :]
-    k_index = jnp.where(valid, panels * panel_rows + a_cols.transpose(1, 2, 3, 0)[0], fine)
-    k_tile = jnp.pad(
-        k_index.astype(BF).reshape(sections * slot_a, rows), ((0, 16 - sections * slot_a), (0, 2 * side - rows))
-    )
+    counts, columns = a_count.transpose(1, 2, 0)[0], a_cols.transpose(1, 2, 3, 0)[0]
+    k_index = [
+        jnp.where(counts > slot, panels[:, :, 0] * panel_rows + columns[:, slot], fine) for slot in range(slot_a)
+    ]
+    k_index = jnp.stack(k_index, axis=1).reshape(sections * slot_a, rows)
+    k_tile = jnp.pad(k_index.astype(BF), ((0, 16 - sections * slot_a), (0, 2 * side - rows)))
     own = jnp.concatenate([a_flat, k_tile], axis=0)
 
     from_left, from_right = swap(own, "col", cols, 1), swap(own, "col", cols, 3)

time: 86.1 us -> 85.9 us (level)
  no operation moved by 1% of the time
where the time goes in v5:
time: 85.9 us; the launch traced here: 85.7 us
  waiting for transfers between devices  38.7 us (45%)
  starting transfers between devices  28 us (33%)
  Pallas kernels  13.6 us (16%)
  other arithmetic  2.99 us (3%)
  local copies, waits for them, and re-layouts  2.15 us (3%)
    ppermute x11, waiting for transfers between devices, swap(): return lax.ppermute(x, axis, [(n, n ^ mask) for n in range(size)])  19.9 us
    ppermute x7, waiting for transfers between devices, shift(): return lax.ppermute(x, axis, [(n, (n + by) % size) for n in range(size)])  18.8 us
    ppermute x11, starting transfers between devices, swap(): return lax.ppermute(x, axis, [(n, n ^ mask) for n in range(size)])  15 us
    ppermute x7, starting transfers between devices, shift(): return lax.ppermute(x, axis, [(n, (n + by) % size) for n in range(size)])  13 us
    pallas_call x1, Pallas kernels, body(): pl.pallas_call(near_kernel, out_shape=sums_shape, in_specs=[VMEM_SPEC] *...  5 us
    pallas_call x1, Pallas kernels, body(): pl.pallas_call(expand_kernel, out_shape=jax.ShapeDtypeStruct((fine + 1, 4...  3.3 us
    pallas_call x1, Pallas kernels, body(): pl.pallas_call(far_kernel, out_shape=[sums_shape, coded, coded], in_specs...  3.2 us
  transfers between devices with their start and end apart: 18, of which 11 were waited for; matrix products, arithmetic and copies ran while one was open for 2% of the time, Pallas kernels for 11%

profile of v5, /device:TPU:8, one launch (start us, length us, event | category | flops | bytes accessed | tf_op | source)
XLA Modules:
  0.0 85.7 jit_solution(15731348085101099651)
XLA Ops:
  2.3 1.2 %fusion.1.refs_0_ = bf16[3088,128]{1,0:T(8,128)(2,1)S(1)} fusion(bf16[4,24]{1,0:T(4,128)(2,1)S(1)} %bitcast.39, bf16[3072,128]{1,0:T(8,128)(2,1)} %bitcast.32), kind=kLoop, calls=%fused_computation.3 | loop fusion | flops 2371584 | bytes 1577152 | tf_op jit(solution)/shard_map/concatenate | solution.py:175
  3.5 1.6 %collective-permute-start.4 = (bf16[3088,128]{1,0:T(8,128)(2,1)S(1)}, bf16[3088,128]{1,0:T(8,128)(2,1)S(1)}, u32[]{:S(2)}, u32[]{:S(2)}) collective-permute-start(bf16[3088,128]{1,0:T(8,128)(2,1)S(1)} %fusion.1.refs_0_), channel_id=1, source_target_pairs={{0,8},{8,0},{16,24},{24,16},{1,9},{9,1},{17,25},{25,17},{2,10},{10... | collective-permute-start | bytes 2371592 | tf_op jit(solution)/shard_map/ppermute | solution.py:147
  5.1 2.1 %collective-permute-start.3 = (bf16[3088,128]{1,0:T(8,128)(2,1)S(1)}, bf16[3088,128]{1,0:T(8,128)(2,1)S(1)}, u32[]{:S(2)}, u32[]{:S(2)}) collective-permute-start(bf16[3088,128]{1,0:T(8,128)(2,1)S(1)} %fusion.1.refs_0_), channel_id=1, source_target_pairs={{0,24},{8,16},{16,8},{24,0},{1,25},{9,17},{17,9},{25,1},{2,26},{10... | collective-permute-start | bytes 2371592 | tf_op jit(solution)/shard_map/ppermute | solution.py:147
  7.6 1.7 %collective-permute-start.2 = (bf16[528,256]{1,0:T(8,128)(2,1)S(1)}, bf16[528,256]{1,0:T(8,128)(2,1)S(1)}, u32[]{:S(2)}, u32[]{:S(2)}) collective-permute-start(bf16[528,256]{1,0:T(8,128)(2,1)S(1)} %get-tuple-element.36), channel_id=1, source_target_pairs={{0,192},{32,224},{64,128},{96,160},{128,64},{160,96},{192,0},{224,... | collective-permute-start | bytes 811016 | tf_op jit(solution)/shard_map/ppermute | solution.py:147
  10.3 1.6 %collective-permute-start = (bf16[528,256]{1,0:T(8,128)(2,1)S(1)}, bf16[528,256]{1,0:T(8,128)(2,1)S(1)}, u32[]{:S(2)}, u32[]{:S(2)}) collective-permute-start(bf16[528,256]{1,0:T(8,128)(2,1)S(1)} %get-tuple-element.36), channel_id=1, source_target_pairs={{0,64},{32,96},{64,0},{96,32},{128,192},{160,224},{192,128},{224,1... | collective-permute-start | bytes 811016 | tf_op jit(solution)/shard_map/ppermute | solution.py:147
  11.8 11.1 %collective-permute-done.4.refs_1_ = bf16[3088,128]{1,0:T(8,128)(2,1)S(1)} collective-permute-done((bf16[3088,128]{1,0:T(8,128)(2,1)S(1)}, bf16[3088,128]{1,0:T(8,128)(2,1)S(1)}, u32[]{:S(2)}, u32[]{:S(2)}) %collective-permute-start.4) | collective-permute-done | bytes 790560 | tf_op jit(solution)/shard_map/ppermute | solution.py:147
  23.0 2.4 %collective-permute-done.3.refs_2_ = bf16[3088,128]{1,0:T(8,128)(2,1)S(1)} collective-permute-done((bf16[3088,128]{1,0:T(8,128)(2,1)S(1)}, bf16[3088,128]{1,0:T(8,128)(2,1)S(1)}, u32[]{:S(2)}, u32[]{:S(2)}) %collective-permute-start.3) | collective-permute-done | bytes 790560 | tf_op jit(solution)/shard_map/ppermute | solution.py:147
  26.8 2.2 %collective-permute-start.7 = (bf16[1552,128]{1,0:T(8,128)(2,1)S(1)}, bf16[1552,128]{1,0:T(8,128)(2,1)S(1)}, u32[]{:S(2)}, u32[]{:S(2)}) collective-permute-start(bf16[1552,128]{1,0:T(8,128)(2,1)S(1)} %slice.19), channel_id=1, source_target_pairs={{0,24},{8,16},{16,8},{24,0},{1,25},{9,17},{17,9},{25,1},{2,26},{10... | collective-permute-start | bytes 1191944 | tf_op jit(solution)/shard_map/ppermute | solution.py:147
  29.4 3.3 %expand.1.refs_3_.dense_ref = bf16[65,4,64,128]{3,2,1,0:T(8,128)(2,1)S(1)} custom-call(s32[1]{0:T(128)} %bitcast.14.row_ref, bf16[4,528,256]{2,1,0:T(8,128)(2,1)S(1)} %pad_maximum_fusion.refs_0_, bf16[4,528,256]{2,1,0:T(8,128)(2,1)S(1)} %collective-permute-done.5.refs_1_), custom_call_target="tpu_custom_call" | custom-call | bytes 10485760 | tf_op jit(solution)/shard_map/expand/pallas_call | solution.py:193
  32.7 5.0 %near.1.sums_in = f32[8,4,48,512]{3,2,1,0:T(8,128)S(1)} custom-call(bf16[3088,128]{1,0:T(8,128)(2,1)S(1)} %fusion.1.refs_0_, bf16[3088,128]{1,0:T(8,128)(2,1)S(1)} %copy-done.1, bf16[3088,128]{1,0:T(8,128)(2,1)S(1)} %copy-done.3, bf16[65,4,64,128]{3,2,1,0:T(8,128)(2,1)S(1)} %expand.1.refs_3_.dense_ref), custom_call_target="tpu_custom_call" | custom-call | flops 4294967296 | bytes 11534336 | tf_op jit(solution)/shard_map/near/pallas_call | solution.py:209
  38.4 1.1 %collective-permute-done.7.second_ref = bf16[1552,128]{1,0:T(8,128)(2,1)S(1)} collective-permute-done((bf16[1552,128]{1,0:T(8,128)(2,1)S(1)}, bf16[1552,128]{1,0:T(8,128)(2,1)S(1)}, u32[]{:S(2)}, u32[]{:S(2)}) %collective-permute-start.7) | collective-permute-done | bytes 397344 | tf_op jit(solution)/shard_map/ppermute | solution.py:147
  39.5 3.2 %far.1 = (f32[8,4,48,512]{3,2,1,0:T(8,128)S(1)}, s16[208,512]{1,0:T(8,128)(2,1)S(1)}, s16[208,512]{1,0:T(8,128)(2,1)S(1)}) custom-call(s32[1]{0:T(128)} %bitcast.1.layer_ref, f32[8,4,48,512]{3,2,1,0:T(8,128)S(1)} %near.1.sums_in, bf16[1536,128]{1,0:T(8,128)(2,1)S(1)} %collective-permute-done.6.first_ref, ...), custom_call_target="tpu_custom_call", output_to_operand_aliasing={{0}: (1, {})} | custom-call | flops 1073741824 | bytes 9437184 | tf_op jit(solution)/shard_map/far/pallas_call | solution.py:219
  42.7 2.0 %collective-permute-start.8 = (s16[208,512]{1,0:T(8,128)(2,1)S(1)}, s16[208,512]{1,0:T(8,128)(2,1)S(1)}, u32[]{:S(2)}, u32[]{:S(2)}) collective-permute-start(s16[208,512]{1,0:T(8,128)(2,1)S(1)} %get-tuple-element.26), channel_id=1, source_target_pairs={{0,1},{1,2},{2,3},{3,4},{4,5},{5,6},{6,7},{7,0},{8,9},{9,10},{10,1... | collective-permute-start | bytes 638984 | tf_op jit(solution)/shard_map/ppermute | solution.py:151
  44.7 4.0 %collective-permute-start.12 = (s16[208,512]{1,0:T(8,128)(2,1)S(1)}, s16[208,512]{1,0:T(8,128)(2,1)S(1)}, u32[]{:S(2)}, u32[]{:S(2)}) collective-permute-start(s16[208,512]{1,0:T(8,128)(2,1)S(1)} %get-tuple-element.28), channel_id=1, source_target_pairs={{0,7},{1,0},{2,1},{3,2},{4,3},{5,4},{6,5},{7,6},{8,15},{9,8},{10,9... | collective-permute-start | bytes 638984 | tf_op jit(solution)/shard_map/ppermute | solution.py:151
  48.7 4.8 %collective-permute-done.8.arrived = s16[208,512]{1,0:T(8,128)(2,1)S(1)} collective-permute-done((s16[208,512]{1,0:T(8,128)(2,1)S(1)}, s16[208,512]{1,0:T(8,128)(2,1)S(1)}, u32[]{:S(2)}, u32[]{:S(2)}) %collective-permute-start.8) | collective-permute-done | bytes 213024 | tf_op jit(solution)/shard_map/ppermute | solution.py:151
  54.2 3.5 %collective-permute-start.13 = (s16[208,512]{1,0:T(8,128)(2,1)S(1)}, s16[208,512]{1,0:T(8,128)(2,1)S(1)}, u32[]{:S(2)}, u32[]{:S(2)}) collective-permute-start(s16[208,512]{1,0:T(8,128)(2,1)S(1)} %hop.8), channel_id=1, source_target_pairs={{0,7},{1,0},{2,1},{3,2},{4,3},{5,4},{6,5},{7,6},{8,15},{9,8},{10,9... | collective-permute-start | bytes 638984 | tf_op jit(solution)/shard_map/ppermute | solution.py:151
  57.6 3.5 %collective-permute-done.9.arrived = s16[208,512]{1,0:T(8,128)(2,1)S(1)} collective-permute-done((s16[208,512]{1,0:T(8,128)(2,1)S(1)}, s16[208,512]{1,0:T(8,128)(2,1)S(1)}, u32[]{:S(2)}, u32[]{:S(2)}) %collective-permute-start.9) | collective-permute-done | bytes 213024 | tf_op jit(solution)/shard_map/ppermute | solution.py:151
  61.8 3.3 %collective-permute-start.14 = (s16[208,512]{1,0:T(8,128)(2,1)S(1)}, s16[208,512]{1,0:T(8,128)(2,1)S(1)}, u32[]{:S(2)}, u32[]{:S(2)}) collective-permute-start(s16[208,512]{1,0:T(8,128)(2,1)S(1)} %hop.9), channel_id=1, source_target_pairs={{0,7},{1,0},{2,1},{3,2},{4,3},{5,4},{6,5},{7,6},{8,15},{9,8},{10,9... | collective-permute-start | bytes 638984 | tf_op jit(solution)/shard_map/ppermute | solution.py:151
  65.1 3.5 %collective-permute-done.10.arrived = s16[208,512]{1,0:T(8,128)(2,1)S(1)} collective-permute-done((s16[208,512]{1,0:T(8,128)(2,1)S(1)}, s16[208,512]{1,0:T(8,128)(2,1)S(1)}, u32[]{:S(2)}, u32[]{:S(2)}) %collective-permute-start.10) | collective-permute-done | bytes 213024 | tf_op jit(solution)/shard_map/ppermute | solution.py:151
  68.9 7.0 %collective-permute-done.11.up = s16[208,512]{1,0:T(8,128)(2,1)S(1)} collective-permute-done((s16[208,512]{1,0:T(8,128)(2,1)S(1)}, s16[208,512]{1,0:T(8,128)(2,1)S(1)}, u32[]{:S(2)}, u32[]{:S(2)}) %collective-permute-start.11) | collective-permute-done | bytes 213024 | tf_op jit(solution)/shard_map/ppermute | solution.py:151
  76.4 3.4 %collective-permute-start.16 = (bf16[48,512]{1,0:T(8,128)(2,1)S(1)}, bf16[48,512]{1,0:T(8,128)(2,1)S(1)}, u32[]{:S(2)}, u32[]{:S(2)}) collective-permute-start(bf16[48,512]{1,0:T(8,128)(2,1)S(1)} %get-tuple-element.31), channel_id=1, source_target_pairs={{0,16},{8,24},{16,0},{24,8},{1,17},{9,25},{17,1},{25,9},{2,18},{10... | collective-permute-start | bytes 147464 | tf_op jit(solution)/shard_map/ppermute | solution.py:147
  79.7 1.1 %collective-permute-start.17 = (bf16[48,512]{1,0:T(8,128)(2,1)S(1)}, bf16[48,512]{1,0:T(8,128)(2,1)S(1)}, u32[]{:S(2)}, u32[]{:S(2)}) collective-permute-start(bf16[48,512]{1,0:T(8,128)(2,1)S(1)} %get-tuple-element.32), channel_id=1, source_target_pairs={{0,24},{8,16},{16,8},{24,0},{1,25},{9,17},{17,9},{25,1},{2,26},{10... | collective-permute-start | bytes 147464 | tf_op jit(solution)/shard_map/ppermute | solution.py:147
  80.9 1.4 %collective-permute-done.16.refs_2_ = bf16[48,512]{1,0:T(8,128)(2,1)S(1)} collective-permute-done((bf16[48,512]{1,0:T(8,128)(2,1)S(1)}, bf16[48,512]{1,0:T(8,128)(2,1)S(1)}, u32[]{:S(2)}, u32[]{:S(2)}) %collective-permute-start.16) | collective-permute-done | bytes 49184 | tf_op jit(solution)/shard_map/ppermute | solution.py:147
  82.3 2.7 %collective-permute-done.17.refs_3_ = bf16[48,512]{1,0:T(8,128)(2,1)S(1)} collective-permute-done((bf16[48,512]{1,0:T(8,128)(2,1)S(1)}, bf16[48,512]{1,0:T(8,128)(2,1)S(1)}, u32[]{:S(2)}, u32[]{:S(2)}) %collective-permute-start.17) | collective-permute-done | bytes 49184 | tf_op jit(solution)/shard_map/ppermute | solution.py:147
  (54 shorter events, 8.9 us)
Async XLA Ops:
  0.0 7.2 %copy-start.6 = (s32[1,1,8,1]{2,3,1,0:T(1,128)S(1)}, s32[1,1,8,1]{2,3,1,0:T(1,128)}, u32[]{:S(2)}) copy-start(s32[1,1,8,1]{2,3,1,0:T(1,128)} %param.15) | copy-start | bytes 100
  0.0 7.2 %copy-start.5 = (s32[1,1,8,1,4]{2,4,3,1,0:T(4,128)S(1)}, s32[1,1,8,1,4]{2,4,3,1,0:T(4,128)}, u32[]{:S(2)}) copy-start(s32[1,1,8,1,4]{2,4,3,1,0:T(4,128)} %param.14) | copy-start | bytes 388
  0.0 7.6 %copy-start.4 = (bf16[1,1,8,1,64,256]{5,4,3,2,1,0:T(8,128)(2,1)S(1)}, bf16[1,1,8,1,64,256]{5,4,3,2,1,0:T(8,128)(2,1)}, u32[]{:S(2)}) copy-start(bf16[1,1,8,1,64,256]{5,4,3,2,1,0:T(8,128)(2,1)} %param.13) | copy-start | bytes 786436
  3.5 19.5 %collective-permute-start.4 = (bf16[3088,128]{1,0:T(8,128)(2,1)S(1)}, bf16[3088,128]{1,0:T(8,128)(2,1)S(1)}, u32[]{:S(2)}, u32[]{:S(2)}) collective-permute-start(bf16[3088,128]{1,0:T(8,128)(2,1)S(1)} %fusion.1.refs_0_), channel_id=1, source_target_pairs={{0,8},{8,0},{16,24},{24,16},{1,9},{9,1},{17,25},{25,17},{2,10},{10... | collective-permute-start | bytes 2371592 | tf_op jit(solution)/shard_map/ppermute | solution.py:147
  5.1 20.3 %collective-permute-start.3 = (bf16[3088,128]{1,0:T(8,128)(2,1)S(1)}, bf16[3088,128]{1,0:T(8,128)(2,1)S(1)}, u32[]{:S(2)}, u32[]{:S(2)}) collective-permute-start(bf16[3088,128]{1,0:T(8,128)(2,1)S(1)} %fusion.1.refs_0_), channel_id=1, source_target_pairs={{0,24},{8,16},{16,8},{24,0},{1,25},{9,17},{17,9},{25,1},{2,26},{10... | collective-permute-start | bytes 2371592 | tf_op jit(solution)/shard_map/ppermute | solution.py:147
  7.6 18.6 %collective-permute-start.2 = (bf16[528,256]{1,0:T(8,128)(2,1)S(1)}, bf16[528,256]{1,0:T(8,128)(2,1)S(1)}, u32[]{:S(2)}, u32[]{:S(2)}) collective-permute-start(bf16[528,256]{1,0:T(8,128)(2,1)S(1)} %get-tuple-element.36), channel_id=1, source_target_pairs={{0,192},{32,224},{64,128},{96,160},{128,64},{160,96},{192,0},{224,... | collective-permute-start | bytes 811016 | tf_op jit(solution)/shard_map/ppermute | solution.py:147
  9.3 16.9 %collective-permute-start.1 = (bf16[528,256]{1,0:T(8,128)(2,1)S(1)}, bf16[528,256]{1,0:T(8,128)(2,1)S(1)}, u32[]{:S(2)}, u32[]{:S(2)}) collective-permute-start(bf16[528,256]{1,0:T(8,128)(2,1)S(1)} %get-tuple-element.36), channel_id=1, source_target_pairs={{0,128},{32,160},{64,192},{96,224},{128,0},{160,32},{192,64},{224,... | collective-permute-start | bytes 811016 | tf_op jit(solution)/shard_map/ppermute | solution.py:147
  10.3 16.0 %collective-permute-start = (bf16[528,256]{1,0:T(8,128)(2,1)S(1)}, bf16[528,256]{1,0:T(8,128)(2,1)S(1)}, u32[]{:S(2)}, u32[]{:S(2)}) collective-permute-start(bf16[528,256]{1,0:T(8,128)(2,1)S(1)} %get-tuple-element.36), channel_id=1, source_target_pairs={{0,64},{32,96},{64,0},{96,32},{128,192},{160,224},{192,128},{224,1... | collective-permute-start | bytes 811016 | tf_op jit(solution)/shard_map/ppermute | solution.py:147
  23.0 3.3 %copy-start = (bf16[3088,128]{1,0:T(8,128)(2,1)}, bf16[3088,128]{1,0:T(8,128)(2,1)S(1)}, u32[]{:S(2)}) copy-start(bf16[3088,128]{1,0:T(8,128)(2,1)S(1)} %collective-permute-done.4.refs_1_) | copy-start | bytes 2371588
  26.6 2.8 %collective-permute-start.5 = (bf16[4,528,256]{2,1,0:T(8,128)(2,1)S(1)}, bf16[4,528,256]{2,1,0:T(8,128)(2,1)S(1)}, u32[]{:S(2)}, u32[]{:S(2)}) collective-permute-start(bf16[4,528,256]{2,1,0:T(8,128)(2,1)S(1)} %pad_maximum_fusion.refs_0_), channel_id=1, source_target_pairs={{0,32},{32,0},{64,96},{96,64},{128,160},{160,128},{192,224},{224,1... | collective-permute-start | bytes 3244040 | tf_op jit(solution)/shard_map/ppermute | solution.py:147
  26.7 11.7 %collective-permute-start.6 = (bf16[1536,128]{1,0:T(8,128)(2,1)}, bf16[1536,128]{1,0:T(8,128)(2,1)S(1)}, u32[]{:S(2)}, u32[]{:S(2)}) collective-permute-start(bf16[1536,128]{1,0:T(8,128)(2,1)} %slice.18), channel_id=1, source_target_pairs={{0,8},{8,0},{16,24},{24,16},{1,9},{9,1},{17,25},{25,17},{2,10},{10... | collective-permute-start | bytes 1179656 | tf_op jit(solution)/shard_map/ppermute | solution.py:147
  26.8 12.7 %collective-permute-start.7 = (bf16[1552,128]{1,0:T(8,128)(2,1)S(1)}, bf16[1552,128]{1,0:T(8,128)(2,1)S(1)}, u32[]{:S(2)}, u32[]{:S(2)}) collective-permute-start(bf16[1552,128]{1,0:T(8,128)(2,1)S(1)} %slice.19), channel_id=1, source_target_pairs={{0,24},{8,16},{16,8},{24,0},{1,25},{9,17},{17,9},{25,1},{2,26},{10... | collective-permute-start | bytes 1191944 | tf_op jit(solution)/shard_map/ppermute | solution.py:147
  29.4 3.3 %copy-start.1 = (bf16[3088,128]{1,0:T(8,128)(2,1)S(1)}, bf16[3088,128]{1,0:T(8,128)(2,1)}, u32[]{:S(2)}) copy-start(bf16[3088,128]{1,0:T(8,128)(2,1)} %copy-done) | copy-start | bytes 2371588
  29.4 3.3 %copy-start.3 = (bf16[3088,128]{1,0:T(8,128)(2,1)S(1)}, bf16[3088,128]{1,0:T(8,128)(2,1)}, u32[]{:S(2)}) copy-start(bf16[3088,128]{1,0:T(8,128)(2,1)} %copy-done.2) | copy-start | bytes 2371588
  42.7 10.8 %collective-permute-start.8 = (s16[208,512]{1,0:T(8,128)(2,1)S(1)}, s16[208,512]{1,0:T(8,128)(2,1)S(1)}, u32[]{:S(2)}, u32[]{:S(2)}) collective-permute-start(s16[208,512]{1,0:T(8,128)(2,1)S(1)} %get-tuple-element.26), channel_id=1, source_target_pairs={{0,1},{1,2},{2,3},{3,4},{4,5},{5,6},{6,7},{7,0},{8,9},{9,10},{10,1... | collective-permute-start | bytes 638984 | tf_op jit(solution)/shard_map/ppermute | solution.py:151
  44.7 9.2 %collective-permute-start.12 = (s16[208,512]{1,0:T(8,128)(2,1)S(1)}, s16[208,512]{1,0:T(8,128)(2,1)S(1)}, u32[]{:S(2)}, u32[]{:S(2)}) collective-permute-start(s16[208,512]{1,0:T(8,128)(2,1)S(1)} %get-tuple-element.28), channel_id=1, source_target_pairs={{0,7},{1,0},{2,1},{3,2},{4,3},{5,4},{6,5},{7,6},{8,15},{9,8},{10,9... | collective-permute-start | bytes 638984 | tf_op jit(solution)/shard_map/ppermute | solution.py:151
  53.8 7.3 %collective-permute-start.9 = (s16[208,512]{1,0:T(8,128)(2,1)S(1)}, s16[208,512]{1,0:T(8,128)(2,1)S(1)}, u32[]{:S(2)}, u32[]{:S(2)}) collective-permute-start(s16[208,512]{1,0:T(8,128)(2,1)S(1)} %hop.5), channel_id=1, source_target_pairs={{0,1},{1,2},{2,3},{3,4},{4,5},{5,6},{6,7},{7,0},{8,9},{9,10},{10,1... | collective-permute-start | bytes 638984 | tf_op jit(solution)/shard_map/ppermute | solution.py:151
  54.2 7.3 %collective-permute-start.13 = (s16[208,512]{1,0:T(8,128)(2,1)S(1)}, s16[208,512]{1,0:T(8,128)(2,1)S(1)}, u32[]{:S(2)}, u32[]{:S(2)}) collective-permute-start(s16[208,512]{1,0:T(8,128)(2,1)S(1)} %hop.8), channel_id=1, source_target_pairs={{0,7},{1,0},{2,1},{3,2},{4,3},{5,4},{6,5},{7,6},{8,15},{9,8},{10,9... | collective-permute-start | bytes 638984 | tf_op jit(solution)/shard_map/ppermute | solution.py:151
  61.4 7.1 %collective-permute-start.10 = (s16[208,512]{1,0:T(8,128)(2,1)S(1)}, s16[208,512]{1,0:T(8,128)(2,1)S(1)}, u32[]{:S(2)}, u32[]{:S(2)}) collective-permute-start(s16[208,512]{1,0:T(8,128)(2,1)S(1)} %hop.6), channel_id=1, source_target_pairs={{0,1},{1,2},{2,3},{3,4},{4,5},{5,6},{6,7},{7,0},{8,9},{9,10},{10,1... | collective-permute-start | bytes 638984 | tf_op jit(solution)/shard_map/ppermute | solution.py:151
  61.8 7.1 %collective-permute-start.14 = (s16[208,512]{1,0:T(8,128)(2,1)S(1)}, s16[208,512]{1,0:T(8,128)(2,1)S(1)}, u32[]{:S(2)}, u32[]{:S(2)}) collective-permute-start(s16[208,512]{1,0:T(8,128)(2,1)S(1)} %hop.9), channel_id=1, source_target_pairs={{0,7},{1,0},{2,1},{3,2},{4,3},{5,4},{6,5},{7,6},{8,15},{9,8},{10,9... | collective-permute-start | bytes 638984 | tf_op jit(solution)/shard_map/ppermute | solution.py:151
  68.8 7.1 %collective-permute-start.11 = (s16[208,512]{1,0:T(8,128)(2,1)S(1)}, s16[208,512]{1,0:T(8,128)(2,1)S(1)}, u32[]{:S(2)}, u32[]{:S(2)}) collective-permute-start(s16[208,512]{1,0:T(8,128)(2,1)S(1)} %hop.7), channel_id=1, source_target_pairs={{0,1},{1,2},{2,3},{3,4},{4,5},{5,6},{6,7},{7,0},{8,9},{9,10},{10,1... | collective-permute-start | bytes 638984 | tf_op jit(solution)/shard_map/ppermute | solution.py:151
  76.1 4.8 %collective-permute-start.15 = (bf16[48,512]{1,0:T(8,128)(2,1)S(1)}, bf16[48,512]{1,0:T(8,128)(2,1)S(1)}, u32[]{:S(2)}, u32[]{:S(2)}) collective-permute-start(bf16[48,512]{1,0:T(8,128)(2,1)S(1)} %get-tuple-element.30), channel_id=1, source_target_pairs={{0,8},{8,0},{16,24},{24,16},{1,9},{9,1},{17,25},{25,17},{2,10},{10... | collective-permute-start | bytes 147464 | tf_op jit(solution)/shard_map/ppermute | solution.py:147
  76.4 6.0 %collective-permute-start.16 = (bf16[48,512]{1,0:T(8,128)(2,1)S(1)}, bf16[48,512]{1,0:T(8,128)(2,1)S(1)}, u32[]{:S(2)}, u32[]{:S(2)}) collective-permute-start(bf16[48,512]{1,0:T(8,128)(2,1)S(1)} %get-tuple-element.31), channel_id=1, source_target_pairs={{0,16},{8,24},{16,0},{24,8},{1,17},{9,25},{17,1},{25,9},{2,18},{10... | collective-permute-start | bytes 147464 | tf_op jit(solution)/shard_map/ppermute | solution.py:147
  79.7 5.3 %collective-permute-start.17 = (bf16[48,512]{1,0:T(8,128)(2,1)S(1)}, bf16[48,512]{1,0:T(8,128)(2,1)S(1)}, u32[]{:S(2)}, u32[]{:S(2)}) collective-permute-start(bf16[48,512]{1,0:T(8,128)(2,1)S(1)} %get-tuple-element.32), channel_id=1, source_target_pairs={{0,24},{8,16},{16,8},{24,0},{1,25},{9,17},{17,9},{25,1},{2,26},{10... | collective-permute-start | bytes 147464 | tf_op jit(solution)/shard_map/ppermute | solution.py:147
  (1 other events, 1.1 us)
